TPU v7x, 128 devices: a whole 4x4x4 slice. The times are simulated.
128 devices in a mesh: row: 4 (over x), col: 32 (over y, z, core).
Axes of the slice: x: 4, y: 4, z: 4, core: 2. Of those that a mesh axis runs over, the one named last changes fastest.
Arguments:
- resident_cell: int32 [8388608], P(('row', 'col')), may hold values from 0 to 16383
- resident_corner: int32 [8388608], P(('row', 'col')), may hold values from 0 to 7
- resident_frac: float32 [3, 8388608], P(None, ('row', 'col')), may hold values from 0 to 0.5
- resident_charge: float32 [8388608], P(('row', 'col')), may hold values from 0.5 to 2
- resident_momentum: float32 [3, 8388608], P(None, ('row', 'col')), may hold values from -6 to 6
- migrant_dest: int32 [262144, 1], P(('row', 'col')), may hold values from 0 to 31; in each aligned block of 2048 rows (0 to 2047, 2048 to 4095, ...) at most 128 rows name the same one
- migrant_cell: int32 [262144], P(('row', 'col')), may hold values from 0 to 16383
- migrant_corner: int32 [262144], P(('row', 'col')), may hold values from 0 to 7
- migrant_frac: float32 [3, 262144], P(None, ('row', 'col')), may hold values from 0 to 0.5
- migrant_charge: float32 [262144], P(('row', 'col')), may hold values from 0.5 to 2
- migrant_momentum: float32 [3, 262144], P(None, ('row', 'col')), may hold values from -6 to 6
- green: bfloat16 [3, 2, 256, 256, 256], P(None, None, ('row', 'col')), may hold values from -6 to 6
Outputs:
- resident_kicked: float32 [3, 8388608], P(None, ('row', 'col'))
- migrant_kicked: float32 [3, 524288], P(None, ('row', 'col'))
Inputs may be any that keep to these rules, and one draw needn't show every extreme that they name: `migrant_dest`: among the rows of one device each destination is named by at most 128 rows, and some device names one destination in exactly 128 of its rows.
All inputs are finite; a program needn't handle non-finite values.
Results may differ from a plain program's by a relative error of at most 0.0003.
Values sent between devices are 32-bit elements; how exact they have to be, the bound alone decides.
A program may use at most 64 MiB of HBM per device.

v0:
```python
import functools

import jax
import jax.numpy as jnp
import numpy as np
from jax import lax
from jax.experimental import pallas as pl
from jax.experimental.pallas import tpu as pltpu
from jax.sharding import PartitionSpec as P

F32, BF, I32 = jnp.float32, jnp.bfloat16, jnp.int32
N_ROW, N_COL = 4, 32
SLOTS = N_ROW * N_COL
ROWS = 208
PAD = 256
BIG = 48 << 20


def split_np(table):
    hi = table.astype(jnp.bfloat16)
    return hi, (table - hi.astype(np.float64)).astype(jnp.bfloat16)


def row_places():
    layer, y = np.full(PAD, -1), np.zeros(PAD, int)
    layer[:192], y[:192] = np.arange(192) // 32, np.arange(192) % 32
    for side in range(2):
        layer[192 + 8 * side : 198 + 8 * side] = np.arange(6)
        y[192 + 8 * side : 200 + 8 * side] = 33 * side - 1
    return layer, y


def tables():
    wave = np.arange(256)
    layer, y = row_places()
    yg = 32 * np.arange(N_ROW)[:, None] + y[None]
    live = ((layer >= 0)[None] & (yg >= 0) & (yg < 128)).reshape(-1, 1)
    angle = 2 * np.pi / 256 * (yg.reshape(-1, 1) * wave % 256)
    ey = np.concatenate([np.cos(angle), np.sin(angle)], axis=1) * live
    zg = (4 * np.arange(N_COL)[None] + np.arange(6)[:, None] - 1).reshape(-1)
    live = ((zg >= 0) & (zg < 128))[None]
    angle = 2 * np.pi / 256 * (wave[:, None] * zg % 256)
    ez = np.stack([np.cos(angle) * live, np.sin(angle) * live])
    ezt = ez.transpose(0, 2, 1).reshape(384, 256)
    x, j = np.arange(128), np.arange(128)
    angle = 2 * np.pi / 256 * (j[:, None] * x % 256)
    imag = -np.sin(angle)
    imag[0] = 1 - 2 * (x % 2)
    dx = np.concatenate([np.cos(angle), imag])
    return [split_np(t) for t in (ey, ez.reshape(512, 192), ezt, dx, dx.T / 256.0**3)]


def split(v):
    hi = v.astype(BF)
    return hi, (v - hi.astype(F32)).astype(BF)


def dot3(a, b, dims=((1,), (0,))):
    one = lambda p, q: lax.dot_general(p, q, (dims, ((), ())), preferred_element_type=F32)
    return one(a[0], b[0]) + (one(a[0], b[1]) + one(a[1], b[0]))


def tile16(row, n):
    return jnp.broadcast_to(row, (16, n)).astype(BF)


def yz_weights(cell, corner, fy, fz, q, n, write):
    y = (cell >> 7) & 31
    z = (cell >> 12) + 1
    yfar = y + ((corner >> 1) & 1) * 2 - 1
    zfar = z + ((corner >> 2) & 1) * 2 - 1
    io8 = lax.broadcasted_iota(I32, (8, n), 0)
    wz = jnp.where(io8 == z, (1.0 - fz) * q, jnp.where(io8 == zfar, fz * q, 0.0))
    near = wz * (1.0 - fy)
    far = wz * fy
    nh = near.astype(BF).astype(F32); nl = near - nh
    fh = far.astype(BF).astype(F32); fl = far - fh
    io16 = lax.broadcasted_iota(I32, (16, n), 0).astype(BF)
    yb = jnp.broadcast_to(y.astype(F32), (16, n)).astype(BF)
    yfb = jnp.broadcast_to(yfar.astype(F32), (16, n)).astype(BF)
    zero = jnp.zeros((16, n), BF)
    masks = [(yb == io16, yfb == io16), (yb == io16 + 16.0, yfb == io16 + 16.0)]
    for ze in range(6):
        a, b, c, d = (tile16(v[ze:ze+1], n) for v in (nh, fh, nl, fl))
        for h in range(2):
            mn, mf = masks[h]
            write(ze*32 + h*16, jnp.where(mn, a, jnp.where(mf, b, zero)), jnp.where(mn, c, jnp.where(mf, d, zero)))
    isb = yfar < 0
    isa = yfar > 31
    rh = jnp.concatenate([jnp.where(isb, fh, 0.0), jnp.where(isa, fh, 0.0)], axis=0).astype(BF)
    rl = jnp.concatenate([jnp.where(isb, fl, 0.0), jnp.where(isa, fl, 0.0)], axis=0).astype(BF)
    write(192, rh, rl)

def deposit_kernel(cell_ref, corner_ref, frac_ref, q_ref, out_ref, a_ref, b_ref, *, n):
    @pl.when(pl.program_id(0) == 0)
    def _():
        out_ref[...] = jnp.zeros_like(out_ref)
    total = cell_ref.shape[-1]
    for s in range(total // n):
        sl = pl.ds(s*n, n)
        cell = cell_ref[:, sl]; corner = corner_ref[:, sl]; q = q_ref[:, sl]
        fx = frac_ref[0:1, sl]; fy = frac_ref[1:2, sl]; fz = frac_ref[2:3, sl]
        def write(r, hi, lo):
            a_ref[r:r+16, sl] = hi
            a_ref[ROWS+r:ROWS+r+16, sl] = lo
        yz_weights(cell, corner, fy, fz, q, n, write)
        x = cell & 127
        xfar = x + (corner & 1)*2 - 1
        gx = 1.0 - fx
        gh = gx.astype(BF).astype(F32); gl = gx - gh
        fh = fx.astype(BF).astype(F32); fl = fx - fh
        io16 = lax.broadcasted_iota(I32, (16, n), 0).astype(BF)
        xb = tile16(x.astype(F32), n); xfb = tile16(xfar.astype(F32), n)
        gh, gl, fh, fl = (tile16(v, n) for v in (gh, gl, fh, fl))
        zero = jnp.zeros((16, n), BF)
        for t in range(8):
            mn = xb == io16 + BF(16*t); mf = xfb == io16 + BF(16*t)
            b_ref[16*t:16*t+16, sl] = jnp.where(mn, gh, jnp.where(mf, fh, zero))
            b_ref[128+16*t:128+16*t+16, sl] = jnp.where(mn, gl, jnp.where(mf, fl, zero))
    out_ref[...] += lax.dot_general(a_ref[...], b_ref[...], (((1,),(1,)),((),())), preferred_element_type=F32)

def deposit(cell, corner, frac, q, blk=2048, n=512):
    total = cell.shape[-1]
    row = pl.BlockSpec((1, blk), lambda i: (0, i))
    return pl.pallas_call(
        functools.partial(deposit_kernel, n=n),
        out_shape=jax.ShapeDtypeStruct((2*ROWS, 256), F32),
        grid=(total//blk,),
        in_specs=[row, row, pl.BlockSpec((3, blk), lambda i: (0, i)), row],
        out_specs=pl.BlockSpec((2*ROWS, 256), lambda i: (0, 0)),
        scratch_shapes=[pltpu.VMEM((2*ROWS, blk), BF), pltpu.VMEM((256, blk), BF)],
        compiler_params=pltpu.CompilerParams(vmem_limit_bytes=48 << 20),
    )(cell.reshape(1, -1), corner.reshape(1, -1), frac, q.reshape(1, -1))

def kick_kernel(ft_ref, cell_ref, corner_ref, frac_ref, q_ref, mom_ref, out_ref, w_ref, *, n):
    total = cell_ref.shape[-1]
    for s in range(total // n):
        sl = pl.ds(s*n, n)
        cell = cell_ref[:, sl]; corner = corner_ref[:, sl]; q = q_ref[:, sl]
        fx = frac_ref[0:1, sl]; fy = frac_ref[1:2, sl]; fz = frac_ref[2:3, sl]
        def write(r, hi, lo):
            w_ref[r:r+16, sl] = hi
            w_ref[ROWS+r:ROWS+r+16, sl] = hi
            w_ref[2*ROWS+r:2*ROWS+r+16, sl] = lo
        yz_weights(cell, corner, fy, fz, q, n, write)
        y = jnp.dot(ft_ref[...], w_ref[:, sl], preferred_element_type=F32)
        x = cell & 127
        xfar = x + (corner & 1)*2 - 1
        io = lax.broadcasted_iota(I32, (128, n), 0)
        wx = jnp.where(io == x, 1.0 - fx, jnp.where(io == xfar, fx, 0.0))
        for a in range(3):
            out_ref[a:a+1, sl] = mom_ref[a:a+1, sl] + jnp.sum(y[a*128:(a+1)*128] * wx, axis=0, keepdims=True)

def kick(ft, cell, corner, frac, q, mom, blk=2048, n=512):
    total = cell.shape[-1]
    row = pl.BlockSpec((1, blk), lambda i: (0, i))
    r3 = pl.BlockSpec((3, blk), lambda i: (0, i))
    return pl.pallas_call(
        functools.partial(kick_kernel, n=n),
        out_shape=jax.ShapeDtypeStruct((3, total), F32),
        grid=(total//blk,),
        in_specs=[pl.BlockSpec(ft.shape, lambda i: (0, 0)), row, row, r3, row, r3],
        out_specs=r3,
        scratch_shapes=[pltpu.VMEM((3*ROWS, blk), BF)],
        compiler_params=pltpu.CompilerParams(vmem_limit_bytes=48 << 20),
    )(ft, cell.reshape(1, -1), corner.reshape(1, -1), frac, q.reshape(1, -1), mom)


def pack_kernel(dest_ref, cell_ref, corner_ref, frac_ref, q_ref, mom_ref, out_ref, lhs_ref):
    total = dest_ref.shape[-1]
    dest = dest_ref[...]
    hits = (lax.broadcasted_iota(I32, (N_COL, total), 0) == dest).astype(F32)
    upper = (lax.broadcasted_iota(I32, (256, 256), 0) < lax.broadcasted_iota(I32, (256, 256), 1)).astype(BF)
    carry = jnp.zeros((N_COL, 1), F32)
    ranks = []
    for s in range(0, total, 256):
        part = hits[:, s : s + 256]
        before = jnp.dot(part.astype(BF), upper, preferred_element_type=F32) + carry
        carry = carry + jnp.sum(part, axis=1, keepdims=True)
        ranks.append(jnp.sum(part * before, axis=0, keepdims=True))
    rank = jnp.concatenate(ranks, axis=1)
    cap = out_ref.shape[-1]
    choose = (lax.broadcasted_iota(I32, (cap, total), 0).astype(F32) == rank).astype(BF)
    payload = jnp.concatenate(
        [
            frac_ref[...],
            q_ref[...],
            mom_ref[...],
            cell_ref[...].astype(F32),
            corner_ref[...].astype(F32),
            jnp.zeros((7, total), F32),
        ],
        axis=0,
    )
    hi = payload.astype(BF)
    rest = payload - hi.astype(F32)
    mid = rest.astype(BF)
    low = (rest - mid.astype(F32)).astype(BF)
    destb = tile16(dest.astype(F32), total)
    zero = jnp.zeros((16, total), BF)
    for d in range(N_COL):
        mask = destb == BF(d)
        for i, piece in enumerate((hi, mid, low)):
            lhs_ref[i * 512 + d * 16 : i * 512 + d * 16 + 16] = jnp.where(mask, piece, zero)
    got = lax.dot_general(lhs_ref[...], choose, (((1,), (1,)), ((), ())), preferred_element_type=F32)
    got = (got[:512] + got[512:1024]) + got[1024:]
    for d in range(N_COL):
        out_ref[d] = got[d * 16 : d * 16 + 9]


def pack(dest, cell, corner, frac, q, mom):
    total = cell.shape[0]
    cap = 2 * total // N_COL
    return pl.pallas_call(
        pack_kernel,
        name="pack",
        out_shape=jax.ShapeDtypeStruct((N_COL, 9, cap), F32),
        scratch_shapes=[pltpu.VMEM((3 * 512, total), BF)],
        compiler_params=pltpu.CompilerParams(vmem_limit_bytes=BIG),
    )(dest.reshape(1, -1), cell.reshape(1, -1), corner.reshape(1, -1), frac, q.reshape(1, -1), mom)


def spread_kernel(first_ref, second_ref, dxh_ref, dxl_ref, out_ref):
    acc = first_ref[...] + second_ref[...]
    grid = (acc[:ROWS, :128] + acc[ROWS:, 128:]) + (acc[:ROWS, 128:] + acc[ROWS:, :128])
    sent = dot3((dxh_ref[...], dxl_ref[...]), split(grid), ((1,), (1,)))
    sent = jnp.concatenate([sent, jnp.zeros((256, PAD - ROWS), F32)], axis=1)
    for part in range(2):
        for half in range(2):
            out_ref[:, 2 * part + half, :] = sent[128 * part : 128 * part + 128, 128 * half : 128 * half + 128]


def spread(first, second, dx):
    return pl.pallas_call(
        spread_kernel,
        name="spread",
        out_shape=jax.ShapeDtypeStruct((SLOTS, 4, 128), F32),
        compiler_params=pltpu.CompilerParams(vmem_limit_bytes=BIG),
    )(first, second, *dx)


def layer_of(shape):
    lane = lax.broadcasted_iota(I32, shape, 1)
    return jnp.where(lane < 192, lane // 32, jnp.where(lane < ROWS, lane % 8, 6))


def solve_kernel(got_ref, green_ref, eyh_ref, eyl_ref, ezh_ref, ezl_ref, zth_ref, ztl_ref, out_ref, lhs_ref, s_ref, q_ref):
    first = (lax.axis_index("row") == 0) & (lax.axis_index("col") == 0)
    layer = layer_of((N_COL, PAD))
    ey = (eyh_ref, eyl_ref)

    @pl.when(pl.program_id(0) == 0)
    def _():
        for part in range(2):
            for r in range(N_ROW):
                rows = slice(32 * r, 32 * r + 32)
                both = jnp.concatenate([got_ref[rows, 2 * part, :], got_ref[rows, 2 * part + 1, :]], axis=1)
                for ze in range(6):
                    hi, lo = split(jnp.where(layer == ze, both, 0.0))
                    where = slice(192 * part + 32 * ze, 192 * part + 32 * ze + 32)
                    lhs_ref[0, where, PAD * r : PAD * r + PAD] = hi
                    lhs_ref[1, where, PAD * r : PAD * r + PAD] = lo
        u = dot3((lhs_ref[0], lhs_ref[1]), (eyh_ref[...], eyl_ref[...]))
        re_c, re_s, im_c, im_s = u[:192, :256], u[:192, 256:], u[192:, :256], u[192:, 256:]
        ez = (ezh_ref[...], ezl_ref[...])

        def forward(real, imag):
            v = dot3(ez, split(jnp.concatenate([real, imag], axis=1)))
            return v[:256, :256] + v[256:, 256:], v[:256, 256:] - v[256:, :256]

        @pl.when(first)
        def _():
            s_ref[0], s_ref[1] = forward(re_c, -re_s)
            s_ref[2], s_ref[3] = forward(im_c, -im_s)

        @pl.when(jnp.logical_not(first))
        def _():
            s_ref[0], s_ref[1] = forward(re_c + im_s, im_c - re_s)

    index = lax.broadcasted_iota(I32, (256, 256), 0) + lax.broadcasted_iota(I32, (256, 256), 1)
    mirror = ((index == 0) | (index == 256)).astype(BF)

    def flip(plane):
        half = jnp.dot(mirror, plane, preferred_element_type=F32).astype(BF)
        return jnp.dot(half, mirror, preferred_element_type=F32)

    def at(part, sign):
        return green_ref[0, part, sign]

    @pl.when(first)
    def _():
        real0 = 0.5 * (at(0, 0).astype(F32) + flip(at(0, 0)))
        imag0 = 0.5 * (at(1, 0).astype(F32) - flip(at(1, 0)))
        real1 = 0.5 * (at(0, 1).astype(F32) + flip(at(0, 1)))
        imag1 = 0.5 * (at(1, 1).astype(F32) - flip(at(1, 1)))
        a_re = s_ref[0] * real0 - s_ref[1] * imag0
        a_im = s_ref[0] * imag0 + s_ref[1] * real0
        b_re = s_ref[2] * real1 - s_ref[3] * imag1
        b_im = s_ref[2] * imag1 + s_ref[3] * real1
        q_ref[0], q_ref[1] = a_re - b_im, a_im + b_re

    @pl.when(jnp.logical_not(first))
    def _():
        real = at(0, 0).astype(F32) + flip(at(0, 1))
        imag = at(1, 0).astype(F32) - flip(at(1, 1))
        q_ref[0] = s_ref[0] * real - s_ref[1] * imag
        q_ref[1] = s_ref[0] * imag + s_ref[1] * real

    q = split(jnp.concatenate([q_ref[0], q_ref[1]], axis=1))
    v = dot3((zth_ref[...], ztl_ref[...]), q)
    v = jnp.concatenate([v[:192, :256] - v[192:, 256:], v[:192, 256:] + v[192:, :256]], axis=0)
    v = split(v)
    for r in range(N_ROW):
        rows = slice(PAD * r, PAD * r + PAD)
        cos = dot3(v, (eyh_ref[rows, :256], eyl_ref[rows, :256]), ((1,), (1,)))
        sin = dot3(v, (eyh_ref[rows, 256:], eyl_ref[rows, 256:]), ((1,), (1,)))
        w = (cos[:192] - sin[192:], cos[192:] + sin[:192])
        for part in range(2):
            mine = jnp.zeros((N_COL, PAD), F32)
            for ze in range(6):
                mine = jnp.where(layer == ze, w[part][32 * ze : 32 * ze + 32], mine)
            for half in range(2):
                out_ref[32 * r : 32 * r + 32, 0, 2 * part + half, :] = mine[:, 128 * half : 128 * half + 128]


def solve(got, green, ey, ez, ezt):
    whole = lambda a: pl.BlockSpec(a.shape, lambda i: (0,) * a.ndim)
    consts = [*ey, *ez, *ezt]
    return pl.pallas_call(
        solve_kernel,
        name="solve",
        out_shape=jax.ShapeDtypeStruct((SLOTS, 3, 4, 128), F32),
        grid=(3,),
        in_specs=[whole(got), pl.BlockSpec((1, 2, 2, 256, 256), lambda i: (i, 0, 0, 0, 0)), *map(whole, consts)],
        out_specs=pl.BlockSpec((SLOTS, 1, 4, 128), lambda i: (0, i, 0, 0)),
        scratch_shapes=[pltpu.VMEM((2, 384, 1024), BF), pltpu.VMEM((4, 256, 256), F32), pltpu.VMEM((2, 256, 256), F32)],
        compiler_params=pltpu.CompilerParams(vmem_limit_bytes=BIG),
    )(got, green, *consts)


def table_kernel(got_ref, xih_ref, xil_ref, out_ref):
    for a in range(3):
        parts = [
            jnp.concatenate([got_ref[:, a, 2 * part, :], got_ref[:, a, 2 * part + 1, :]], axis=1) for part in range(2)
        ]
        field = dot3((xih_ref[...], xil_ref[...]), split(jnp.concatenate(parts, axis=0)))
        hi, lo = split(field[:, :ROWS])
        out_ref[128 * a : 128 * a + 128] = jnp.concatenate([hi, lo, hi], axis=1)


def table(got, xi):
    return pl.pallas_call(
        table_kernel,
        name="table",
        out_shape=jax.ShapeDtypeStruct((384, 3 * ROWS), BF),
        compiler_params=pltpu.CompilerParams(vmem_limit_bytes=BIG),
    )(got, *xi)


def body(
    resident_cell,
    resident_corner,
    resident_frac,
    resident_charge,
    resident_momentum,
    migrant_dest,
    migrant_cell,
    migrant_corner,
    migrant_frac,
    migrant_charge,
    migrant_momentum,
    green,
):
    ey, ez, ezt, dx, xi = [tuple(map(jnp.asarray, pair)) for pair in tables()]
    packed = pack(
        migrant_dest.reshape(-1), migrant_cell, migrant_corner, migrant_frac, migrant_charge, migrant_momentum
    )
    arrived = lax.all_to_all(packed, "col", 0, 0, tiled=True)
    arrived = arrived.transpose(1, 0, 2).reshape(9, -1)
    moved = (arrived[7].astype(I32), arrived[8].astype(I32), arrived[0:3], arrived[3])
    stayed = (resident_cell, resident_corner, resident_frac, resident_charge)
    sent = spread(deposit(*stayed), deposit(*moved), dx)
    got = lax.all_to_all(sent, ("row", "col"), 0, 0, tiled=True)
    sent = solve(got, green, ey, ez, ezt)
    got = lax.all_to_all(sent, ("row", "col"), 0, 0, tiled=True)
    field = table(got, xi)
    return kick(field, *stayed, resident_momentum), kick(field, *moved, arrived[4:7])


def solution(mesh):
    both = ("row", "col")
    in_specs = (
        P(both),
        P(both),
        P(None, both),
        P(both),
        P(None, both),
        P(both, None),
        P(both),
        P(both),
        P(None, both),
        P(both),
        P(None, both),
        P(None, None, both, None, None),
    )
    out_specs = (P(None, both), P(None, both))
    return jax.shard_map(body, mesh=mesh, in_specs=in_specs, out_specs=out_specs, check_vma=False)
```

profile of v0, /device:TPU:1, one launch (start us, length us, event | category | flops | bytes accessed | tf_op | source)
XLA Modules:
  0.0 157.1 jit_solution(12199556618351117532)
XLA Ops:
  0.6 0.0 copy-start.20
  0.6 0.7 copy-done.20
  1.4 0.8 copy-done.21
  2.2 0.7 copy-done.22
  2.8 0.7 copy-done.23
  3.5 0.7 copy-done.24
  4.2 0.7 copy-done.25
  4.9 2.8 %pack.1 = f32[32,9,128]{2,1,0:T(8,128)} custom-call(s32[1,2048]{1,0:T(1,128)S(1)} %bitcast.24, s32[1,2048]{1,0:T(1,128)S(1)} %bitcast.25, s32[1,2048]{1,0:T(1,128)S(1)} %bitcast.26, f32[3,2048]{1,0:T(4,128)S(1)} %copy-done.20, f32[1,2048]{1,0:T(1,128)S(1)} %bitcast.27, f32[3,2048]{1,0:T(4,128)S(1)} %copy-done.21), custom_call_target="tpu_custom_call" | custom-call | tf_op jit(solution)/shard_map/pack/pallas_call | solution.py:214
  7.7 9.7 %all-to-all-start = ((f32[32,9,128]{2,1,0:T(8,128)}), f32[32,9,128]{2,1,0:T(8,128)}, u32[]{:S(2)}, u32[]{:S(2)}) async-start(f32[32,9,128]{2,1,0:T(8,128)} %pack.1), calls=%async_computation | async-start | bytes 524288 | tf_op jit(solution)/shard_map/all_to_all | solution.py:378
  17.4 0.0 copy-start
  17.4 1.2 copy-done
  18.6 0.9 copy-done.3
  19.5 0.9 copy-done.5
  20.5 0.9 copy-done.7
  21.4 23.2 %shard_map.221.first_ref = f32[416,256]{1,0:T(8,128)S(1)} custom-call(s32[1,65536]{1,0:T(1,128)S(1)} %bitcast.18, s32[1,65536]{1,0:T(1,128)S(1)} %bitcast.20, f32[3,65536]{1,0:T(4,128)S(1)} %copy-done, f32[1,65536]{1,0:T(1,128)S(1)} %bitcast.22), custom_call_target="tpu_custom_call" | custom-call | tf_op jit(solution)/shard_map/pallas_call | solution.py:125
  44.7 0.0 copy-start.2
  44.7 0.0 copy-start.10
  44.7 0.0 all-to-all-done
  44.7 1.2 slice_bitcast_fusion.2
  45.9 1.0 slice_bitcast_fusion
  46.9 1.5 shard_map.222.second_ref
  48.4 0.0 copy-start.16
  48.4 0.8 copy-done.16
  49.3 0.8 copy-done.19
  50.1 0.4 spread.1
  50.5 20.0 %all_to_all.15.got_ref = f32[128,4,128]{2,1,0:T(4,128)S(1)} all-to-all(f32[128,4,128]{2,1,0:T(4,128)S(1)} %spread.1), channel_id=1, replica_groups=mesh['row'=4,'col'=32] {'row','col'}, dimensions={0} | all-to-all | bytes 524288 | tf_op jit(solution)/shard_map/all_to_all | solution.py:383
  70.6 0.0 copy-done.12
  70.6 0.0 copy-done.14
  70.6 0.0 copy-done.2
  70.6 0.0 copy-done.10
  70.6 0.0 copy-start.11
  70.6 1.2 copy-done.11
  71.8 0.9 copy-done.13
  72.8 0.9 copy-done.15
  73.7 9.1 %solve.1 = f32[128,3,4,128]{3,2,1,0:T(4,128)S(1)} custom-call(f32[128,4,128]{2,1,0:T(4,128)S(1)} %all_to_all.15.got_ref, bf16[3,2,2,256,256]{4,3,2,1,0:T(8,128)(2,1)S(1)} %copy-done.2, bf16[1024,512]{1,0:T(8,128)(2,1)S(1)} %copy-done.11, bf16[1024,512]{1,0:T(8,128)(2,1)S(1)} %copy-done.10, bf16[512,192]{1,0:T(8,128)(2,1)S(1)} %copy-done.13, ...), custom_call_target="tpu_custom_call" | custom-call | tf_op jit(solution)/shard_map/solve/pallas_call | solution.py:329
  82.8 0.0 copy-start.1
  82.8 0.0 copy-start.4
  82.8 0.0 copy-start.6
  82.8 0.0 copy-start.8
  82.8 0.0 copy-start.9
  82.9 21.6 %all_to_all.16.got_ref = f32[128,3,4,128]{3,2,1,0:T(4,128)S(1)} all-to-all(f32[128,3,4,128]{3,2,1,0:T(4,128)S(1)} %solve.1), channel_id=1, replica_groups=mesh['row'=4,'col'=32] {'row','col'}, dimensions={0} | all-to-all | bytes 1572864 | tf_op jit(solution)/shard_map/all_to_all | solution.py:385
  104.5 0.0 copy-done.17
  104.5 0.0 copy-done.18
  104.5 0.8 table.1.ft_ref
  105.3 3.6 %shard_map.224 = f32[3,4096]{1,0:T(4,128)} custom-call(bf16[384,624]{1,0:T(8,128)(2,1)S(1)} %table.1.ft_ref, s32[1,4096]{1,0:T(1,128)S(1)} %get-tuple-element.6.cell_ref, s32[1,4096]{1,0:T(1,128)S(1)} %get-tuple-element.5.corner_ref, f32[3,4096]{1,0:T(4,128)S(1)} %get-tuple-element.3.frac_ref, f32[1,4096]{1,0:T(1,128)S(1)} %get-tuple-element.4.q_ref, ...), custom_call_target="tpu_custom_call" | custom-call | tf_op jit(solution)/shard_map/pallas_call | solution.py:158
  108.9 0.0 copy-done.1
  108.9 0.0 copy-done.6
  108.9 48.2 %shard_map.223 = f32[3,65536]{1,0:T(4,128)} custom-call(bf16[384,624]{1,0:T(8,128)(2,1)S(1)} %table.1.ft_ref, s32[1,65536]{1,0:T(1,128)S(1)} %bitcast.19, s32[1,65536]{1,0:T(1,128)S(1)} %bitcast.21, f32[3,65536]{1,0:T(4,128)S(1)} %copy-done.1, f32[1,65536]{1,0:T(1,128)S(1)} %bitcast.23, f32[3,65536]{1,0:T(4,128)S(1)} %copy-done.9), custom_call_target="tpu_custom_call" | custom-call | tf_op jit(solution)/shard_map/pallas_call | solution.py:158
  (18 shorter events, 0.0 us)
Async XLA Ops:
  0.6 0.8 copy-start.20
  1.4 0.8 copy-start.21
  2.1 0.7 copy-start.22
  2.8 0.7 copy-start.23
  3.5 0.7 copy-start.24
  4.2 0.7 copy-start.25
  7.7 37.0 %all-to-all-start = ((f32[32,9,128]{2,1,0:T(8,128)}), f32[32,9,128]{2,1,0:T(8,128)}, u32[]{:S(2)}, u32[]{:S(2)}) async-start(f32[32,9,128]{2,1,0:T(8,128)} %pack.1), calls=%async_computation | async-start | bytes 524288 | tf_op jit(solution)/shard_map/all_to_all | solution.py:378
  17.4 1.2 copy-start
  18.6 0.9 copy-start.3
  19.5 0.9 copy-start.5
  20.5 0.9 copy-start.7
  21.4 49.1 %copy-start.12 = (bf16[512,192]{1,0:T(8,128)(2,1)S(1)}, bf16[512,192]{1,0:T(8,128)(2,1)}, u32[]{:S(2)}) copy-start(bf16[512,192]{1,0:T(8,128)(2,1)} %constant.23.clone.ezl_ref) | copy-start | bytes 589828
  21.4 49.1 %copy-start.14 = (bf16[384,256]{1,0:T(8,128)(2,1)S(1)}, bf16[384,256]{1,0:T(8,128)(2,1)}, u32[]{:S(2)}) copy-start(bf16[384,256]{1,0:T(8,128)(2,1)} %constant.25.clone.ztl_ref) | copy-start | bytes 589828
  44.7 25.9 %copy-start.2 = (bf16[3,2,2,256,256]{4,3,2,1,0:T(8,128)(2,1)S(1)}, bf16[3,2,2,256,256]{4,3,2,1,0:T(8,128)(2,1)}, u32[]{:S(2)}) copy-start(bf16[3,2,2,256,256]{4,3,2,1,0:T(8,128)(2,1)} %green_ref.1) | copy-start | bytes 4718596
  44.7 25.9 %copy-start.10 = (bf16[1024,512]{1,0:T(8,128)(2,1)S(1)}, bf16[1024,512]{1,0:T(8,128)(2,1)}, u32[]{:S(2)}) copy-start(bf16[1024,512]{1,0:T(8,128)(2,1)} %constant.21.clone.eyl_ref) | copy-start | bytes 3145732
  48.4 0.8 copy-start.16
  49.3 0.8 copy-start.19
  70.6 1.2 copy-start.11
  71.8 0.9 copy-start.13
  72.8 0.9 copy-start.15
  73.7 30.8 %copy-start.17 = (bf16[128,256]{1,0:T(8,128)(2,1)S(1)}, bf16[128,256]{1,0:T(8,128)(2,1)}, u32[]{:S(2)}) copy-start(bf16[128,256]{1,0:T(8,128)(2,1)} %constant.29.clone.xil_ref) | copy-start | bytes 196612
  73.7 30.8 %copy-start.18 = (bf16[128,256]{1,0:T(8,128)(2,1)S(1)}, bf16[128,256]{1,0:T(8,128)(2,1)}, u32[]{:S(2)}) copy-start(bf16[128,256]{1,0:T(8,128)(2,1)} %constant.28.clone.xih_ref) | copy-start | bytes 196612
  82.8 26.1 %copy-start.1 = (f32[3,65536]{1,0:T(4,128)S(1)}, f32[3,65536]{1,0:T(4,128)}, u32[]{:S(2)}) copy-start(f32[3,65536]{1,0:T(4,128)} %frac_ref.5) | copy-start | bytes 2359300
  82.8 26.1 %copy-start.4 = (s32[65536]{0:T(1024)S(1)}, s32[65536]{0:T(1024)}, u32[]{:S(2)}) copy-start(s32[65536]{0:T(1024)} %param.22) | copy-start | bytes 786436
  82.8 26.1 %copy-start.6 = (s32[65536]{0:T(1024)S(1)}, s32[65536]{0:T(1024)}, u32[]{:S(2)}) copy-start(s32[65536]{0:T(1024)} %param.23) | copy-start | bytes 786436
  82.8 26.0 %copy-start.8 = (f32[65536]{0:T(1024)S(1)}, f32[65536]{0:T(1024)}, u32[]{:S(2)}) copy-start(f32[65536]{0:T(1024)} %param.25) | copy-start | bytes 786436
  82.8 26.0 %copy-start.9 = (f32[3,65536]{1,0:T(4,128)S(1)}, f32[3,65536]{1,0:T(4,128)}, u32[]{:S(2)}) copy-start(f32[3,65536]{1,0:T(4,128)} %mom_ref.3) | copy-start | bytes 2359300
where the time goes:
time: 158 us; the launch traced here: 157 us
  Pallas kernels  89.5 us (57%)
  blocking collectives  41.6 us (26%)
  local copies, waits for them, and re-layouts  14.2 us (9%)
  starting transfers between devices  9.66 us (6%)
    pallas_call x2, Pallas kernels, kick(): pl.pallas_call(functools.partial(kick_kernel, n=n), out_shape=jax.ShapeDt...  51.8 us
    all_to_all x2, blocking collectives, body(): got = lax.all_to_all(sent, ('row', 'col'), 0, 0, tiled=True)  41.6 us
    pallas_call x2, Pallas kernels, deposit(): pl.pallas_call(functools.partial(deposit_kernel, n=n), out_shape=jax.Shap...  24.7 us
    unnamed x52, local copies, waits for them, and re-layouts  13.2 us
    all_to_all x1, starting transfers between devices, body(): arrived = lax.all_to_all(packed, 'col', 0, 0, tiled=True)  9.66 us
    pallas_call x1, Pallas kernels, solve(): pl.pallas_call(solve_kernel, name='solve', out_shape=jax.ShapeDtypeStruct...  9.1 us
  transfers between devices with their start and end apart: 1, of which 0 were waited for; matrix products, arithmetic and copies ran while one was open for 0% of the time, Pallas kernels for 15%

commit v1 on v0

v1 whole, which is shorter than its diff:
```python
import functools

import jax
import jax.numpy as jnp
import numpy as np
from jax import lax
from jax.experimental import pallas as pl
from jax.experimental.pallas import tpu as pltpu
from jax.sharding import PartitionSpec as P

F32, BF, I32 = jnp.float32, jnp.bfloat16, jnp.int32
N_ROW, N_COL = 4, 32
SLOTS = N_ROW * N_COL
ROWS = 208
PAD = 256
BIG = 48 << 20


def split_np(table):
    hi = table.astype(jnp.bfloat16)
    return hi, (table - hi.astype(np.float64)).astype(jnp.bfloat16)


def row_places():
    layer, y = np.full(PAD, -1), np.zeros(PAD, int)
    layer[:192], y[:192] = np.arange(192) // 32, np.arange(192) % 32
    for side in range(2):
        layer[192 + 8 * side : 198 + 8 * side] = np.arange(6)
        y[192 + 8 * side : 200 + 8 * side] = 33 * side - 1
    return layer, y


def tables():
    wave = np.arange(256)
    layer, y = row_places()
    yg = 32 * np.arange(N_ROW)[:, None] + y[None]
    live = ((layer >= 0)[None] & (yg >= 0) & (yg < 128)).reshape(-1, 1)
    angle = 2 * np.pi / 256 * (yg.reshape(-1, 1) * wave % 256)
    ey = np.concatenate([np.cos(angle), np.sin(angle)], axis=1) * live
    zg = (4 * np.arange(N_COL)[None] + np.arange(6)[:, None] - 1).reshape(-1)
    live = ((zg >= 0) & (zg < 128))[None]
    angle = 2 * np.pi / 256 * (wave[:, None] * zg % 256)
    ez = np.stack([np.cos(angle) * live, np.sin(angle) * live])
    ezt = ez.transpose(0, 2, 1).reshape(384, 256)
    x, j = np.arange(128), np.arange(128)
    angle = 2 * np.pi / 256 * (j[:, None] * x % 256)
    imag = -np.sin(angle)
    imag[0] = 1 - 2 * (x % 2)
    dx = np.concatenate([np.cos(angle), imag])
    return [split_np(t) for t in (ey, ez.reshape(512, 192), ezt, dx, dx.T / 256.0**3)]


def split(v):
    hi = v.astype(BF)
    return hi, (v - hi.astype(F32)).astype(BF)


def dot3(a, b, dims=((1,), (0,))):
    one = lambda p, q: lax.dot_general(p, q, (dims, ((), ())), preferred_element_type=F32)
    return one(a[0], b[0]) + (one(a[0], b[1]) + one(a[1], b[0]))


def tile16(row, n):
    return jnp.broadcast_to(row, (16, n)).astype(BF)


def yz_weights(cell, corner, fy, fz, q, n, write):
    y = (cell >> 7) & 31
    z = (cell >> 12) + 1
    yfar = y + ((corner >> 1) & 1) * 2 - 1
    zfar = z + ((corner >> 2) & 1) * 2 - 1
    io8 = lax.broadcasted_iota(I32, (8, n), 0)
    wz = jnp.where(io8 == z, (1.0 - fz) * q, jnp.where(io8 == zfar, fz * q, 0.0))
    near = wz * (1.0 - fy)
    far = wz * fy
    nh = near.astype(BF).astype(F32); nl = near - nh
    fh = far.astype(BF).astype(F32); fl = far - fh
    io16 = lax.broadcasted_iota(I32, (16, n), 0).astype(BF)
    yb = jnp.broadcast_to(y.astype(F32), (16, n)).astype(BF)
    yfb = jnp.broadcast_to(yfar.astype(F32), (16, n)).astype(BF)
    zero = jnp.zeros((16, n), BF)
    masks = [(yb == io16, yfb == io16), (yb == io16 + 16.0, yfb == io16 + 16.0)]
    for ze in range(6):
        a, b, c, d = (tile16(v[ze:ze+1], n) for v in (nh, fh, nl, fl))
        for h in range(2):
            mn, mf = masks[h]
            write(ze*32 + h*16, jnp.where(mn, a, jnp.where(mf, b, zero)), jnp.where(mn, c, jnp.where(mf, d, zero)))
    isb = yfar < 0
    isa = yfar > 31
    rh = jnp.concatenate([jnp.where(isb, fh, 0.0), jnp.where(isa, fh, 0.0)], axis=0).astype(BF)
    rl = jnp.concatenate([jnp.where(isb, fl, 0.0), jnp.where(isa, fl, 0.0)], axis=0).astype(BF)
    write(192, rh, rl)

def x_weights(cell, corner, fx, n, write):
    x = cell & 127
    xfar = x + (corner & 1) * 2 - 1
    gx = 1.0 - fx
    gh = gx.astype(BF).astype(F32)
    fh = fx.astype(BF).astype(F32)
    gh, gl, fh, fl = (tile16(v, n) for v in (gh, gx - gh, fh, fx - fh))
    io16 = lax.broadcasted_iota(I32, (16, n), 0).astype(BF)
    xb, xfb = tile16(x.astype(F32), n), tile16(xfar.astype(F32), n)
    zero = jnp.zeros((16, n), BF)
    for t in range(8):
        near, far = xb == io16 + BF(16 * t), xfb == io16 + BF(16 * t)
        write(16 * t, jnp.where(near, gh, jnp.where(far, fh, zero)), jnp.where(near, gl, jnp.where(far, fl, zero)))


def deposit_block(rows, a_ref, b_ref, acc_ref, n):
    for s in range(a_ref.shape[1] // n):
        here = pl.ds(s * n, n)
        cell, corner, fx, fy, fz, q = rows(s)

        def write_a(r, hi, lo):
            a_ref[r : r + 16, here] = hi
            a_ref[ROWS + r : ROWS + r + 16, here] = lo

        def write_b(r, hi, lo):
            b_ref[r : r + 16, here] = hi
            b_ref[128 + r : 128 + r + 16, here] = lo

        yz_weights(cell, corner, fy, fz, q, n, write_a)
        x_weights(cell, corner, fx, n, write_b)
    acc_ref[...] += lax.dot_general(a_ref[...], b_ref[...], (((1,), (1,)), ((), ())), preferred_element_type=F32)


def pack_into(dest_ref, cell_ref, corner_ref, frac_ref, q_ref, mom_ref, lhs_ref, out_ref):
    total = dest_ref.shape[-1]
    dest = dest_ref[...]
    hits = (lax.broadcasted_iota(I32, (N_COL, total), 0) == dest).astype(F32)
    upper = (lax.broadcasted_iota(I32, (256, 256), 0) < lax.broadcasted_iota(I32, (256, 256), 1)).astype(BF)
    carry = jnp.zeros((N_COL, 1), F32)
    ranks = []
    for s in range(0, total, 256):
        part = hits[:, s : s + 256]
        before = jnp.dot(part.astype(BF), upper, preferred_element_type=F32) + carry
        carry = carry + jnp.sum(part, axis=1, keepdims=True)
        ranks.append(jnp.sum(part * before, axis=0, keepdims=True))
    rank = jnp.concatenate(ranks, axis=1)
    cap = out_ref.shape[-1]
    choose = (lax.broadcasted_iota(I32, (cap, total), 0).astype(F32) == rank).astype(BF)
    payload = jnp.concatenate(
        [
            frac_ref[...],
            q_ref[...],
            mom_ref[...],
            cell_ref[...].astype(F32),
            corner_ref[...].astype(F32),
            jnp.zeros((7, total), F32),
        ],
        axis=0,
    )
    hi = payload.astype(BF)
    rest = payload - hi.astype(F32)
    mid = rest.astype(BF)
    low = (rest - mid.astype(F32)).astype(BF)
    destb = tile16(dest.astype(F32), total)
    zero = jnp.zeros((16, total), BF)
    for d in range(N_COL):
        mask = destb == BF(d)
        for i, piece in enumerate((hi, mid, low)):
            lhs_ref[i * 512 + d * 16 : i * 512 + d * 16 + 16] = jnp.where(mask, piece, zero)
    got = lax.dot_general(lhs_ref[...], choose, (((1,), (1,)), ((), ())), preferred_element_type=F32)
    got = (got[:512] + got[512:1024]) + got[1024:]
    for d in range(N_COL):
        out_ref[d] = got[d * 16 : d * 16 + 9]


def kick_kernel(ft_ref, cell_ref, corner_ref, frac_ref, q_ref, mom_ref, out_ref, w_ref, *, n):
    total = cell_ref.shape[-1]
    for s in range(total // n):
        sl = pl.ds(s*n, n)
        cell = cell_ref[:, sl]; corner = corner_ref[:, sl]; q = q_ref[:, sl]
        fx = frac_ref[0:1, sl]; fy = frac_ref[1:2, sl]; fz = frac_ref[2:3, sl]
        def write(r, hi, lo):
            w_ref[r:r+16, sl] = hi
            w_ref[ROWS+r:ROWS+r+16, sl] = hi
            w_ref[2*ROWS+r:2*ROWS+r+16, sl] = lo
        yz_weights(cell, corner, fy, fz, q, n, write)
        y = jnp.dot(ft_ref[...], w_ref[:, sl], preferred_element_type=F32)
        x = cell & 127
        xfar = x + (corner & 1)*2 - 1
        io = lax.broadcasted_iota(I32, (128, n), 0)
        wx = jnp.where(io == x, 1.0 - fx, jnp.where(io == xfar, fx, 0.0))
        for a in range(3):
            out_ref[a:a+1, sl] = mom_ref[a:a+1, sl] + jnp.sum(y[a*128:(a+1)*128] * wx, axis=0, keepdims=True)

def kick(ft, cell, corner, frac, q, mom, blk=2048, n=512):
    total = cell.shape[-1]
    row = pl.BlockSpec((1, blk), lambda i: (0, i))
    r3 = pl.BlockSpec((3, blk), lambda i: (0, i))
    return pl.pallas_call(
        functools.partial(kick_kernel, n=n),
        out_shape=jax.ShapeDtypeStruct((3, total), F32),
        grid=(total//blk,),
        in_specs=[pl.BlockSpec(ft.shape, lambda i: (0, 0)), row, row, r3, row, r3],
        out_specs=r3,
        scratch_shapes=[pltpu.VMEM((3*ROWS, blk), BF)],
        compiler_params=pltpu.CompilerParams(vmem_limit_bytes=48 << 20),
    )(ft, cell.reshape(1, -1), corner.reshape(1, -1), frac, q.reshape(1, -1), mom)


def layer_of(shape):
    lane = lax.broadcasted_iota(I32, shape, 1)
    return jnp.where(lane < 192, lane // 32, jnp.where(lane < ROWS, lane % 8, 6))


def green_into(green_ref, h_ref, first):
    index = lax.broadcasted_iota(I32, (256, 256), 0) + lax.broadcasted_iota(I32, (256, 256), 1)
    mirror = ((index == 0) | (index == 256)).astype(BF)

    def flip(plane):
        half = jnp.dot(mirror, plane, preferred_element_type=F32).astype(BF)
        return jnp.dot(half, mirror, preferred_element_type=F32)

    @pl.when(first)
    def _():
        for a in range(3):
            for sign in range(2):
                real, imag = green_ref[a, 0, sign], green_ref[a, 1, sign]
                h_ref[a, 2 * sign] = 0.5 * (real.astype(F32) + flip(real))
                h_ref[a, 2 * sign + 1] = 0.5 * (imag.astype(F32) - flip(imag))

    @pl.when(jnp.logical_not(first))
    def _():
        for a in range(3):
            h_ref[a, 0] = green_ref[a, 0, 0].astype(F32) + flip(green_ref[a, 0, 1])
            h_ref[a, 1] = green_ref[a, 1, 0].astype(F32) - flip(green_ref[a, 1, 1])


def forward_into(got_ref, ey, ez, lhs_ref, s_ref, first):
    layer = layer_of((N_COL, PAD))
    for part in range(2):
        for r in range(N_ROW):
            rows = slice(32 * r, 32 * r + 32)
            both = jnp.concatenate([got_ref[rows, 2 * part, :], got_ref[rows, 2 * part + 1, :]], axis=1)
            for ze in range(6):
                hi, lo = split(jnp.where(layer == ze, both, 0.0))
                where = slice(192 * part + 32 * ze, 192 * part + 32 * ze + 32)
                lhs_ref[0, where, PAD * r : PAD * r + PAD] = hi
                lhs_ref[1, where, PAD * r : PAD * r + PAD] = lo
    u = dot3((lhs_ref[0], lhs_ref[1]), (ey[0][...], ey[1][...]))
    re_c, re_s, im_c, im_s = u[:192, :256], u[:192, 256:], u[192:, :256], u[192:, 256:]
    ezs = (ez[0][...], ez[1][...])

    def forward(real, imag):
        v = dot3(ezs, split(jnp.concatenate([real, imag], axis=1)))
        return v[:256, :256] + v[256:, 256:], v[:256, 256:] - v[256:, :256]

    @pl.when(first)
    def _():
        s_ref[0], s_ref[1] = forward(re_c, -re_s)
        s_ref[2], s_ref[3] = forward(im_c, -im_s)

    @pl.when(jnp.logical_not(first))
    def _():
        s_ref[0], s_ref[1] = forward(re_c + im_s, im_c - re_s)


def back_into(a, h_ref, s_ref, q_ref, zt, ey, out_ref, first):
    layer = layer_of((N_COL, PAD))
    a_re = s_ref[0] * h_ref[a, 0] - s_ref[1] * h_ref[a, 1]
    a_im = s_ref[0] * h_ref[a, 1] + s_ref[1] * h_ref[a, 0]
    q_ref[0], q_ref[1] = a_re, a_im

    @pl.when(first)
    def _():
        b_re = s_ref[2] * h_ref[a, 2] - s_ref[3] * h_ref[a, 3]
        b_im = s_ref[2] * h_ref[a, 3] + s_ref[3] * h_ref[a, 2]
        q_ref[0] = q_ref[0] - b_im
        q_ref[1] = q_ref[1] + b_re

    q = split(jnp.concatenate([q_ref[0], q_ref[1]], axis=1))
    v = dot3((zt[0][...], zt[1][...]), q)
    v = jnp.concatenate([v[:192, :256] - v[192:, 256:], v[:192, 256:] + v[192:, :256]], axis=0)
    v = split(v)
    for r in range(N_ROW):
        rows = slice(PAD * r, PAD * r + PAD)
        cos = dot3(v, (ey[0][rows, :256], ey[1][rows, :256]), ((1,), (1,)))
        sin = dot3(v, (ey[0][rows, 256:], ey[1][rows, 256:]), ((1,), (1,)))
        w = (cos[:192] - sin[192:], cos[192:] + sin[:192])
        for part in range(2):
            mine = jnp.zeros((N_COL, PAD), F32)
            for ze in range(6):
                mine = jnp.where(layer == ze, w[part][32 * ze : 32 * ze + 32], mine)
            for half in range(2):
                out_ref[a, 32 * r : 32 * r + 32, 2 * part + half, :] = mine[:, 128 * half : 128 * half + 128]


MESH = pl.DeviceIdType.MESH
N_IN = 21


def field_kernel(*refs, n):
    hbm, (table_ref, moved_ref) = refs[:N_IN], refs[N_IN : N_IN + 2]
    held = refs[N_IN + 2 : 2 * N_IN + 2]
    (lhs_p, pack_s, pack_r, a_ref, b_ref, acc_ref, send1, recv1, h_ref, lhs_f, s_ref, q_ref, send2, recv2) = refs[
        2 * N_IN + 2 : 2 * N_IN + 16
    ]
    in_sem, own_sem, ss_m, rs_m, ss_1, rs_1, ss_2, rs_2 = refs[2 * N_IN + 16 :]
    row, col = lax.axis_index("row"), lax.axis_index("col")
    me = row * N_COL + col
    first = me == 0

    def device(d):
        return (d >> 5, d & 31)

    copies = [pltpu.make_async_copy(h, v, in_sem.at[i]) for i, (h, v) in enumerate(zip(hbm, held))]
    for copy in copies:
        copy.start()

    barrier = pltpu.get_barrier_semaphore()

    def greet(i, _):
        pl.semaphore_signal(barrier, inc=1, device_id=device((me + i) & 127), device_id_type=MESH)
        return 0

    lax.fori_loop(1, SLOTS, greet, 0)
    acc_ref[...] = jnp.zeros_like(acc_ref)

    for copy in copies[:6]:
        copy.wait()
    pack_into(*held[:6], lhs_p, pack_s)
    for copy in copies[6:10]:
        copy.wait()
    cell_ref, corner_ref, frac_ref, q_in = held[6:10]
    blk = a_ref.shape[1]
    steps = cell_ref.shape[1] // blk

    def resident(i, _):
        def rows(s):
            here = pl.ds(pl.multiple_of(i * blk + s * n, n), n)
            return (
                cell_ref[:, here],
                corner_ref[:, here],
                frac_ref[0:1, here],
                frac_ref[1:2, here],
                frac_ref[2:3, here],
                q_in[:, here],
            )

        deposit_block(rows, a_ref, b_ref, acc_ref, n)
        return 0

    lax.fori_loop(0, steps // 2, resident, 0)
    pl.semaphore_wait(barrier, SLOTS - 1)

    def send_migrants(i, _):
        c = (col + i) & 31
        pltpu.make_async_remote_copy(
            src_ref=pack_s.at[c],
            dst_ref=pack_r.at[col],
            send_sem=ss_m,
            recv_sem=rs_m,
            device_id=(row, c),
            device_id_type=MESH,
        ).start()
        return 0

    lax.fori_loop(1, N_COL, send_migrants, 0)
    own = pltpu.make_async_copy(pack_s.at[col], pack_r.at[col], own_sem.at[0])
    own.start()
    lax.fori_loop(steps // 2, steps, resident, 0)
    own.wait()
    rest = pl.ds(0, N_COL - 1)
    pltpu.make_async_remote_copy(
        src_ref=pack_s.at[rest],
        dst_ref=pack_r.at[rest],
        send_sem=ss_m,
        recv_sem=rs_m,
        device_id=(row, col),
        device_id_type=MESH,
    ).wait()
    for s in range(N_COL):
        moved_ref[:, 128 * s : 128 * s + 128] = pack_r[s]

    def migrant(i, _):
        def rows(s):
            here = pl.ds(pl.multiple_of(i * blk + s * n, n), n)
            got = moved_ref[:, here]
            return (
                got[7:8].astype(I32),
                got[8:9].astype(I32),
                got[0:1],
                got[1:2],
                got[2:3],
                got[3:4],
            )

        deposit_block(rows, a_ref, b_ref, acc_ref, n)
        return 0

    lax.fori_loop(0, moved_ref.shape[1] // blk, migrant, 0)
    for copy in copies[10:]:
        copy.wait()
    green_ref = held[10]
    ey, ez, zt, dx, xi = (held[11 + 2 * i : 13 + 2 * i] for i in range(5))

    acc = acc_ref[...]
    grid = (acc[:ROWS, :128] + acc[ROWS:, 128:]) + (acc[:ROWS, 128:] + acc[ROWS:, :128])
    sent = dot3((dx[0][...], dx[1][...]), split(grid), ((1,), (1,)))
    sent = jnp.concatenate([sent, jnp.zeros((256, PAD - ROWS), F32)], axis=1)
    for part in range(2):
        for half in range(2):
            send1[:, 2 * part + half, :] = sent[128 * part : 128 * part + 128, 128 * half : 128 * half + 128]

    def exchange(src, dst, ss, rs, own_at):
        def go(i, _):
            d = (me + i) & 127
            pltpu.make_async_remote_copy(
                src_ref=src.at[d],
                dst_ref=dst.at[me],
                send_sem=ss,
                recv_sem=rs,
                device_id=device(d),
                device_id_type=MESH,
            ).start()
            return 0

        lax.fori_loop(1, SLOTS, go, 0)
        own = pltpu.make_async_copy(src.at[me], dst.at[me], own_at)
        own.start()
        return own

    def finish(own, src, dst, ss, rs):
        own.wait()
        rest = pl.ds(0, SLOTS - 1)
        pltpu.make_async_remote_copy(
            src_ref=src.at[rest],
            dst_ref=dst.at[rest],
            send_sem=ss,
            recv_sem=rs,
            device_id=(row, col),
            device_id_type=MESH,
        ).wait()

    own = exchange(send1, recv1, ss_1, rs_1, own_sem.at[1])
    green_into(green_ref, h_ref, first)
    finish(own, send1, recv1, ss_1, rs_1)
    forward_into(recv1, ey, ez, lhs_f, s_ref, first)
    owns = []
    for a in range(3):
        back_into(a, h_ref, s_ref, q_ref, zt, ey, send2, first)
        owns.append(exchange(send2.at[a], recv2.at[a], ss_2.at[a], rs_2.at[a], own_sem.at[2 + a]))
    for a in range(3):
        finish(owns[a], send2.at[a], recv2.at[a], ss_2.at[a], rs_2.at[a])
        parts = [jnp.concatenate([recv2[a, :, 2 * part, :], recv2[a, :, 2 * part + 1, :]], axis=1) for part in range(2)]
        field = dot3((xi[0][...], xi[1][...]), split(jnp.concatenate(parts, axis=0)))
        hi, lo = split(field[:, :ROWS])
        table_ref[128 * a : 128 * a + 128] = jnp.concatenate([hi, lo, hi], axis=1)


def field_of(operands, blk=2048, n=512):
    ops = [o.reshape(1, -1) if o.ndim == 1 else o for o in operands]
    assert len(ops) == N_IN
    cap = 128
    dma = pltpu.SemaphoreType.DMA
    return pl.pallas_call(
        functools.partial(field_kernel, n=n),
        name="field",
        out_shape=(jax.ShapeDtypeStruct((384, 3 * ROWS), BF), jax.ShapeDtypeStruct((9, N_COL * cap), F32)),
        in_specs=[pl.BlockSpec(memory_space=pltpu.MemorySpace.HBM)] * N_IN,
        out_specs=(pl.BlockSpec(memory_space=pltpu.VMEM),) * 2,
        scratch_shapes=[pltpu.VMEM(o.shape, o.dtype) for o in ops]
        + [
            pltpu.VMEM((3 * 512, ops[0].shape[1]), BF),
            pltpu.VMEM((N_COL, 9, cap), F32),
            pltpu.VMEM((N_COL, 9, cap), F32),
            pltpu.VMEM((2 * ROWS, blk), BF),
            pltpu.VMEM((256, blk), BF),
            pltpu.VMEM((2 * ROWS, 256), F32),
            pltpu.VMEM((SLOTS, 4, 128), F32),
            pltpu.VMEM((SLOTS, 4, 128), F32),
            pltpu.VMEM((3, 4, 256, 256), F32),
            pltpu.VMEM((2, 384, 1024), BF),
            pltpu.VMEM((4, 256, 256), F32),
            pltpu.VMEM((2, 256, 256), F32),
            pltpu.VMEM((3, SLOTS, 4, 128), F32),
            pltpu.VMEM((3, SLOTS, 4, 128), F32),
            dma((N_IN,)),
            dma((5,)),
            dma(()),
            dma(()),
            dma(()),
            dma(()),
            dma((3,)),
            dma((3,)),
        ],
        compiler_params=pltpu.CompilerParams(vmem_limit_bytes=56 << 20, has_side_effects=True, collective_id=0),
    )(*ops)


def body(
    resident_cell,
    resident_corner,
    resident_frac,
    resident_charge,
    resident_momentum,
    migrant_dest,
    migrant_cell,
    migrant_corner,
    migrant_frac,
    migrant_charge,
    migrant_momentum,
    green,
):
    consts = [jnp.asarray(t) for pair in tables() for t in pair]
    stayed = (resident_cell, resident_corner, resident_frac, resident_charge)
    field, moved = field_of(
        [
            migrant_dest.reshape(-1),
            migrant_cell,
            migrant_corner,
            migrant_frac,
            migrant_charge,
            migrant_momentum,
            *stayed,
            green,
            *consts,
        ]
    )
    went = (moved[7].astype(I32), moved[8].astype(I32), moved[0:3], moved[3])
    return kick(field, *stayed, resident_momentum), kick(field, *went, moved[4:7])


def solution(mesh):
    both = ("row", "col")
    in_specs = (
        P(both),
        P(both),
        P(None, both),
        P(both),
        P(None, both),
        P(both, None),
        P(both),
        P(both),
        P(None, both),
        P(both),
        P(None, both),
        P(None, None, both, None, None),
    )
    out_specs = (P(None, both), P(None, both))
    return jax.shard_map(body, mesh=mesh, in_specs=in_specs, out_specs=out_specs, check_vma=False)
```

time: 158 us -> 121 us (0.77)
  blocking collectives: 41.6 us -> 0 us
  Pallas kernels: 89.5 us -> 115 us
  local copies, waits for them, and re-layouts: 14.2 us -> 3.07 us
  starting transfers between devices: 9.66 us -> 0 us
    all_to_all x2 -> x0, blocking collectives: 41.6 us -> none  [body(): got = lax.all_to_all(sent, ('row', 'col'), 0, 0, tiled=True)]
    pallas_call x6 -> x1, Pallas kernels: 37.7 us -> 63.7 us  [field_of(): pl.pallas_call(functools.partial(field_kernel, n=n), name='field', out_sh...]
    unnamed x52 -> x14, local copies, waits for them, and re-layouts: 13.2 us -> 2.07 us
    all_to_all x1 -> x0, starting transfers between devices: 9.66 us -> none  [body(): arrived = lax.all_to_all(packed, 'col', 0, 0, tiled=True)]
  transfers between devices with their start and end apart: 1 -> 0, of which waited for: 0 -> 0; matrix products, arithmetic and copies ran while one was open for 0% -> 0% of each run, Pallas kernels for 15% -> 0%
where the time goes in v1:
time: 121 us; the launch traced here: 120 us
  Pallas kernels  115 us (95%)
  local copies, waits for them, and re-layouts  3.07 us (3%)
    pallas_call x1, Pallas kernels, field_of(): pl.pallas_call(functools.partial(field_kernel, n=n), name='field', out_sh...  63.7 us
    pallas_call x2, Pallas kernels, kick(): pl.pallas_call(functools.partial(kick_kernel, n=n), out_shape=jax.ShapeDt...  51.6 us

profile of v1, /device:TPU:1, one launch (start us, length us, event | category | flops | bytes accessed | tf_op | source)
XLA Modules:
  0.0 120.3 jit_solution(3850669304347850120)
XLA Ops:
  0.6 0.0 copy-start.3
  0.6 0.0 copy-start.4
  0.7 0.0 copy-start.5
  0.7 0.0 copy-start.6
  0.7 63.7 %field.1 = (bf16[384,624]{1,0:T(8,128)(2,1)}, f32[9,4096]{1,0:T(8,128)}) custom-call(s32[1,2048]{1,0:T(1,128)} %bitcast.13, s32[1,2048]{1,0:T(1,128)} %bitcast.14, s32[1,2048]{1,0:T(1,128)} %bitcast.15, f32[3,2048]{1,0:T(4,128)} %refs_3_.1, f32[1,2048]{1,0:T(1,128)} %bitcast.16, f32[3,2048]{1,0:T(4,128)} %refs_5_.1, s32[1,65536]{1,0:T(1,128)} %bitcast.7, ...), custom_call_target="tpu_custom_call" | custom-call | tf_op jit(solution)/shard_map/field/pallas_call | solution.py:458
  64.4 0.0 copy-start
  64.4 1.2 fusion.1
  65.5 1.0 fusion
  66.5 0.0 copy-start.1
  66.5 1.0 copy-done.1
  67.6 3.6 %shard_map.222 = f32[3,4096]{1,0:T(4,128)} custom-call(bf16[384,624]{1,0:T(8,128)(2,1)S(1)} %copy-done.1, s32[1,4096]{1,0:T(1,128)S(1)} %get-tuple-element.10.cell_ref, s32[1,4096]{1,0:T(1,128)S(1)} %get-tuple-element.9.corner_ref, f32[3,4096]{1,0:T(4,128)S(1)} %get-tuple-element.7.frac_ref, f32[1,4096]{1,0:T(1,128)S(1)} %get-tuple-element.8.q_ref, ...), custom_call_target="tpu_custom_call" | custom-call | tf_op jit(solution)/shard_map/pallas_call | solution.py:192
  71.2 0.0 copy-done.3
  71.2 0.0 copy-done.4
  71.2 0.0 copy-done.5
  71.2 0.0 copy-done.6
  71.2 0.0 copy-done
  71.2 0.0 copy-start.2
  71.2 1.0 copy-done.2
  72.2 48.0 %shard_map.221 = f32[3,65536]{1,0:T(4,128)} custom-call(bf16[384,624]{1,0:T(8,128)(2,1)S(1)} %copy-done.2, s32[1,65536]{1,0:T(1,128)S(1)} %bitcast.8, s32[1,65536]{1,0:T(1,128)S(1)} %bitcast.10, f32[3,65536]{1,0:T(4,128)S(1)} %copy-done, f32[1,65536]{1,0:T(1,128)S(1)} %bitcast.12, f32[3,65536]{1,0:T(4,128)S(1)} %copy-done.6), custom_call_target="tpu_custom_call" | custom-call | tf_op jit(solution)/shard_map/pallas_call | solution.py:192
Async XLA Ops:
  0.6 70.5 %copy-start.3 = (s32[65536]{0:T(1024)S(1)}, s32[65536]{0:T(1024)}, u32[]{:S(2)}) copy-start(s32[65536]{0:T(1024)} %param.22) | copy-start | bytes 786436
  0.6 70.5 %copy-start.4 = (s32[65536]{0:T(1024)S(1)}, s32[65536]{0:T(1024)}, u32[]{:S(2)}) copy-start(s32[65536]{0:T(1024)} %param.23) | copy-start | bytes 786436
  0.7 70.5 %copy-start.5 = (f32[65536]{0:T(1024)S(1)}, f32[65536]{0:T(1024)}, u32[]{:S(2)}) copy-start(f32[65536]{0:T(1024)} %param.25) | copy-start | bytes 786436
  0.7 70.5 %copy-start.6 = (f32[3,65536]{1,0:T(4,128)S(1)}, f32[3,65536]{1,0:T(4,128)}, u32[]{:S(2)}) copy-start(f32[3,65536]{1,0:T(4,128)} %mom_ref.1) | copy-start | bytes 2359300
  64.4 6.8 %copy-start = (f32[3,65536]{1,0:T(4,128)S(1)}, f32[3,65536]{1,0:T(4,128)}, u32[]{:S(2)}) copy-start(f32[3,65536]{1,0:T(4,128)} %frac_ref.1) | copy-start | bytes 2359300
  66.5 1.0 copy-start.1
  71.2 1.0 copy-start.2

commit v2 on v1

--- a/solution.py
+++ b/solution.py
@@ -8,12 +8,12 @@
 from jax.experimental.pallas import tpu as pltpu
 from jax.sharding import PartitionSpec as P
 
-F32, BF, I32 = jnp.float32, jnp.bfloat16, jnp.int32
+F32, BF, I32, F8 = jnp.float32, jnp.bfloat16, jnp.int32, jnp.float8_e4m3fn
 N_ROW, N_COL = 4, 32
 SLOTS = N_ROW * N_COL
 ROWS = 208
 PAD = 256
-BIG = 48 << 20
+BIG = 60 << 20
 
 
 def split_np(table):
@@ -166,38 +166,141 @@
         out_ref[d] = got[d * 16 : d * 16 + 9]
 
 
-def kick_kernel(ft_ref, cell_ref, corner_ref, frac_ref, q_ref, mom_ref, out_ref, w_ref, *, n):
-    total = cell_ref.shape[-1]
-    for s in range(total // n):
-        sl = pl.ds(s*n, n)
-        cell = cell_ref[:, sl]; corner = corner_ref[:, sl]; q = q_ref[:, sl]
-        fx = frac_ref[0:1, sl]; fy = frac_ref[1:2, sl]; fz = frac_ref[2:3, sl]
-        def write(r, hi, lo):
-            w_ref[r:r+16, sl] = hi
-            w_ref[ROWS+r:ROWS+r+16, sl] = hi
-            w_ref[2*ROWS+r:2*ROWS+r+16, sl] = lo
-        yz_weights(cell, corner, fy, fz, q, n, write)
-        y = jnp.dot(ft_ref[...], w_ref[:, sl], preferred_element_type=F32)
-        x = cell & 127
-        xfar = x + (corner & 1)*2 - 1
-        io = lax.broadcasted_iota(I32, (128, n), 0)
-        wx = jnp.where(io == x, 1.0 - fx, jnp.where(io == xfar, fx, 0.0))
-        for a in range(3):
-            out_ref[a:a+1, sl] = mom_ref[a:a+1, sl] + jnp.sum(y[a*128:(a+1)*128] * wx, axis=0, keepdims=True)
-
-def kick(ft, cell, corner, frac, q, mom, blk=2048, n=512):
-    total = cell.shape[-1]
-    row = pl.BlockSpec((1, blk), lambda i: (0, i))
-    r3 = pl.BlockSpec((3, blk), lambda i: (0, i))
+def yz_tiles(cell, corner, fy, fz, q, n, write):
+    y = (cell >> 7) & 31
+    z = (cell >> 12) + 1
+    yfar = y + ((corner >> 1) & 1) * 2 - 1
+    zfar = z + ((corner >> 2) & 1) * 2 - 1
+    io8 = lax.broadcasted_iota(I32, (8, n), 0)
+    wz = jnp.where(io8 == z, (1.0 - fz) * q, jnp.where(io8 == zfar, fz * q, 0.0))
+    near = wz * (1.0 - fy)
+    far = wz * fy
+    nh = near.astype(BF).astype(F32)
+    fh = far.astype(BF).astype(F32)
+    nl, fl = (near - nh) * 4096.0, (far - fh) * 4096.0
+
+    def big(row):
+        half = tile16(row, n)
+        return jnp.concatenate([half, half], axis=0)
+
+    io = lax.broadcasted_iota(I32, (32, n), 0).astype(F32).astype(BF)
+    at_near, at_far = big(y.astype(F32)) == io, big(yfar.astype(F32)) == io
+    zero = jnp.zeros((32, n), BF)
+    for ze in range(6):
+        a, b, c, d = (big(v[ze : ze + 1]) for v in (nh, fh, nl, fl))
+        write(ze * 32, jnp.where(at_near, a, jnp.where(at_far, b, zero)), jnp.where(at_near, c, jnp.where(at_far, d, zero)))
+    below, above = yfar < 0, yfar > 31
+    rims = [
+        jnp.concatenate([jnp.where(below, v, 0.0), jnp.where(above, v, 0.0), jnp.zeros((16, n), F32)], axis=0)
+        for v in (fh, fl)
+    ]
+    write(192, rims[0].astype(BF), rims[1].astype(BF))
+
+
+def kick_chunk(ft_ref, f8_ref, w_ref, w8_ref, here, n, rows):
+    cell, corner, fx, fy, fz, q = rows
+
+    def write(r, hi, lo):
+        w_ref[r : r + 32, here] = hi
+        w8_ref[r : r + 32, here] = hi.astype(F8)
+        w8_ref[PAD + r : PAD + r + 32, here] = lo.astype(F8)
+
+    yz_tiles(cell, corner, fy, fz, q, n, write)
+    got = jnp.dot(ft_ref[...], w_ref[:, here], preferred_element_type=F32)
+    more = jnp.dot(f8_ref[...], w8_ref[:, here], preferred_element_type=F32)
+    x = cell & 127
+    xfar = x + (corner & 1) * 2 - 1
+    io = lax.broadcasted_iota(I32, (128, n), 0)
+    wx = jnp.where(io == x, 1.0 - fx, jnp.where(io == xfar, fx, 0.0))
+    total = got + more
+    return [jnp.sum(total[a * 128 : a * 128 + 128] * wx, axis=0, keepdims=True) for a in range(3)]
+
+
+def kick_kernel(*refs, n):
+    hbm, (out_hbm, migrant_ref), held = refs[:9], refs[9:11], refs[11:20]
+    out_ref, w_ref, w8_ref, made_sem, in_sem, out_sem = refs[20:]
+    made = [pltpu.make_async_copy(hbm[i], held[i], made_sem.at[i]) for i in range(4)]
+    for copy in made:
+        copy.start()
+    (ft_ref, f8_ref, scale_ref, moved_ref), hbm, held = held[:4], hbm[4:], held[4:]
+    cell_ref, corner_ref, frac_ref, q_ref, mom_ref = held
+    blk = w_ref.shape[1]
+    total = cell_ref.shape[1]
+    pieces = (pl.ds(0, blk), pl.ds(blk, total - blk))
+    copies = [
+        [pltpu.make_async_copy(h.at[:, p], v.at[:, p], in_sem.at[j, i]) for i, (h, v) in enumerate(zip(hbm, held))]
+        for j, p in enumerate(pieces)
+    ]
+    for copy in copies[0] + copies[1]:
+        copy.start()
+    for r in (224, 480):
+        w8_ref[r : r + 32] = jnp.zeros((32, blk), F8)
+    w_ref[224:] = jnp.zeros((32, blk), BF)
+    chunk = functools.partial(kick_chunk, ft_ref, f8_ref, w_ref, w8_ref)
+    for copy in made:
+        copy.wait()
+
+    def migrants(i, _):
+        for s in range(blk // n):
+            here = pl.ds(pl.multiple_of(i * blk + s * n, n), n)
+            got = moved_ref[:, here]
+            rows = (got[7:8].astype(I32), got[8:9].astype(I32), got[0:1], got[1:2], got[2:3], got[3:4])
+            kicks = chunk(pl.ds(s * n, n), n, rows)
+            for a in range(3):
+                migrant_ref[a : a + 1, here] = got[4 + a : 5 + a] + kicks[a] * scale_ref[a : a + 1, 0:1]
+        return 0
+
+    lax.fori_loop(0, moved_ref.shape[1] // blk, migrants, 0)
+    for copy in copies[0]:
+        copy.wait()
+
+    def residents(i, _):
+        @pl.when(i == 1)
+        def _():
+            for copy in copies[1]:
+                copy.wait()
+
+        for s in range(blk // n):
+            here = pl.ds(pl.multiple_of(i * blk + s * n, n), n)
+            rows = (
+                cell_ref[:, here],
+                corner_ref[:, here],
+                frac_ref[0:1, here],
+                frac_ref[1:2, here],
+                frac_ref[2:3, here],
+                q_ref[:, here],
+            )
+            kicks = chunk(pl.ds(s * n, n), n, rows)
+            for a in range(3):
+                out_ref[a : a + 1, here] = mom_ref[a : a + 1, here] + kicks[a] * scale_ref[a : a + 1, 0:1]
+        block = pl.ds(pl.multiple_of(i * blk, blk), blk)
+        pltpu.make_async_copy(out_ref.at[:, block], out_hbm.at[:, block], out_sem).start()
+        return 0
+
+    lax.fori_loop(0, total // blk, residents, 0)
+    pltpu.make_async_copy(out_ref, out_hbm, out_sem).wait()
+
+
+def kick(tables_of, moved, cell, corner, frac, q, mom, blk=4096, n=256):
+    ops = [*tables_of, moved, cell.reshape(1, -1), corner.reshape(1, -1), frac, q.reshape(1, -1), mom]
+    vmem, hbm = (pl.BlockSpec(memory_space=s) for s in (pltpu.VMEM, pltpu.MemorySpace.HBM))
     return pl.pallas_call(
         functools.partial(kick_kernel, n=n),
-        out_shape=jax.ShapeDtypeStruct((3, total), F32),
-        grid=(total//blk,),
-        in_specs=[pl.BlockSpec(ft.shape, lambda i: (0, 0)), row, row, r3, row, r3],
-        out_specs=r3,
-        scratch_shapes=[pltpu.VMEM((3*ROWS, blk), BF)],
-        compiler_params=pltpu.CompilerParams(vmem_limit_bytes=48 << 20),
-    )(ft, cell.reshape(1, -1), corner.reshape(1, -1), frac, q.reshape(1, -1), mom)
+        name="kick",
+        out_shape=(jax.ShapeDtypeStruct(mom.shape, F32), jax.ShapeDtypeStruct((3, moved.shape[1]), F32)),
+        in_specs=[hbm] * 9,
+        out_specs=(hbm, vmem),
+        scratch_shapes=[pltpu.VMEM(o.shape, o.dtype) for o in ops]
+        + [
+            pltpu.VMEM(mom.shape, F32),
+            pltpu.VMEM((PAD, blk), BF),
+            pltpu.VMEM((2 * PAD, blk), F8),
+            pltpu.SemaphoreType.DMA((4,)),
+            pltpu.SemaphoreType.DMA((2, 5)),
+            pltpu.SemaphoreType.DMA(()),
+        ],
+        compiler_params=pltpu.CompilerParams(vmem_limit_bytes=BIG),
+    )(*ops)
 
 
 def layer_of(shape):
@@ -292,12 +395,12 @@
 
 
 def field_kernel(*refs, n):
-    hbm, (table_ref, moved_ref) = refs[:N_IN], refs[N_IN : N_IN + 2]
-    held = refs[N_IN + 2 : 2 * N_IN + 2]
+    hbm, (ft_ref, f8_ref, scale_ref, moved_ref) = refs[:N_IN], refs[N_IN : N_IN + 4]
+    held = refs[N_IN + 4 : 2 * N_IN + 4]
     (lhs_p, pack_s, pack_r, a_ref, b_ref, acc_ref, send1, recv1, h_ref, lhs_f, s_ref, q_ref, send2, recv2) = refs[
-        2 * N_IN + 2 : 2 * N_IN + 16
+        2 * N_IN + 4 : 2 * N_IN + 18
     ]
-    in_sem, own_sem, ss_m, rs_m, ss_1, rs_1, ss_2, rs_2 = refs[2 * N_IN + 16 :]
+    in_sem, own_sem, ss_m, rs_m, ss_1, rs_1, ss_2, rs_2 = refs[2 * N_IN + 18 :]
     row, col = lax.axis_index("row"), lax.axis_index("col")
     me = row * N_COL + col
     first = me == 0
@@ -446,8 +549,16 @@
         finish(owns[a], send2.at[a], recv2.at[a], ss_2.at[a], rs_2.at[a])
         parts = [jnp.concatenate([recv2[a, :, 2 * part, :], recv2[a, :, 2 * part + 1, :]], axis=1) for part in range(2)]
         field = dot3((xi[0][...], xi[1][...]), split(jnp.concatenate(parts, axis=0)))
-        hi, lo = split(field[:, :ROWS])
-        table_ref[128 * a : 128 * a + 128] = jnp.concatenate([hi, lo, hi], axis=1)
+        top = jnp.max(jnp.max(jnp.abs(field), axis=0, keepdims=True), axis=1, keepdims=True)
+        top = jnp.maximum(top, 1e-30)
+        field = field / top
+        hi = field.astype(BF).astype(F32)
+        here = slice(128 * a, 128 * a + 128)
+        ft_ref[here] = (hi * 65536.0).astype(BF)
+        f8_ref[here, :PAD] = ((field - hi) * 65536.0).astype(F8)
+        f8_ref[here, PAD:] = (hi * 16.0).astype(F8)
+        scale_ref[a : a + 1] = jnp.broadcast_to(top * (1.0 / 65536.0), (1, 128))
+    scale_ref[3:] = jnp.zeros((5, 128), F32)
 
 
 def field_of(operands, blk=2048, n=512):
@@ -458,9 +569,14 @@
     return pl.pallas_call(
         functools.partial(field_kernel, n=n),
         name="field",
-        out_shape=(jax.ShapeDtypeStruct((384, 3 * ROWS), BF), jax.ShapeDtypeStruct((9, N_COL * cap), F32)),
+        out_shape=(
+            jax.ShapeDtypeStruct((384, PAD), BF),
+            jax.ShapeDtypeStruct((384, 2 * PAD), F8),
+            jax.ShapeDtypeStruct((8, 128), F32),
+            jax.ShapeDtypeStruct((9, N_COL * cap), F32),
+        ),
         in_specs=[pl.BlockSpec(memory_space=pltpu.MemorySpace.HBM)] * N_IN,
-        out_specs=(pl.BlockSpec(memory_space=pltpu.VMEM),) * 2,
+        out_specs=(pl.BlockSpec(memory_space=pltpu.VMEM),) * 4,
         scratch_shapes=[pltpu.VMEM(o.shape, o.dtype) for o in ops]
         + [
             pltpu.VMEM((3 * 512, ops[0].shape[1]), BF),
@@ -486,7 +602,7 @@
             dma((3,)),
             dma((3,)),
         ],
-        compiler_params=pltpu.CompilerParams(vmem_limit_bytes=56 << 20, has_side_effects=True, collective_id=0),
+        compiler_params=pltpu.CompilerParams(vmem_limit_bytes=BIG, has_side_effects=True, collective_id=0),
     )(*ops)
 
 
@@ -506,7 +622,7 @@
 ):
     consts = [jnp.asarray(t) for pair in tables() for t in pair]
     stayed = (resident_cell, resident_corner, resident_frac, resident_charge)
-    field, moved = field_of(
+    *field, moved = field_of(
         [
             migrant_dest.reshape(-1),
             migrant_cell,
@@ -519,8 +635,7 @@
             *consts,
         ]
     )
-    went = (moved[7].astype(I32), moved[8].astype(I32), moved[0:3], moved[3])
-    return kick(field, *stayed, resident_momentum), kick(field, *went, moved[4:7])
+    return kick(field, moved, *stayed, resident_momentum)
 
 
 def solution(mesh):

time: 121 us -> 104 us (0.86)
  Pallas kernels: 115 us -> 103 us
  local copies, waits for them, and re-layouts: 3.07 us -> 0 us
    pallas_call x2 -> x1, Pallas kernels: 51.6 us -> 38.9 us  [kick(): pl.pallas_call(functools.partial(kick_kernel, n=n), name='kick', out_shap...]
    unnamed x14 -> x0, local copies, waits for them, and re-layouts: 2.07 us -> none
where the time goes in v2:
time: 104 us; the launch traced here: 103 us
  Pallas kernels  103 us (99%)
    pallas_call x1, Pallas kernels, field_of(): pl.pallas_call(functools.partial(field_kernel, n=n), name='field', out_sh...  63.7 us
    pallas_call x1, Pallas kernels, kick(): pl.pallas_call(functools.partial(kick_kernel, n=n), name='kick', out_shap...  38.9 us

profile of v2, /device:TPU:1, one launch (start us, length us, event | category | flops | bytes accessed | tf_op | source)
XLA Modules:
  0.0 103.4 jit_solution(8853070195321347382)
XLA Ops:
  0.6 63.7 %field.1 = (bf16[384,256]{1,0:T(8,128)(2,1)}, f8e4m3fn[384,512]{1,0:T(32,128)(4,1)}, f32[8,128]{1,0:T(8,128)}, f32[9,4096]{1,0:T(8,128)}) custom-call(s32[1,2048]{1,0:T(1,128)} %bitcast.13, s32[1,2048]{1,0:T(1,128)} %bitcast.14, s32[1,2048]{1,0:T(1,128)} %bitcast.15, f32[3,2048]{1,0:T(4,128)} %refs_3_.1, f32[1,2048]{1,0:T(1,128)} %bitcast.16, ...), custom_call_target="tpu_custom_call" | custom-call | tf_op jit(solution)/shard_map/field/pallas_call | solution.py:569
  64.4 38.9 %kick.1 = (f32[3,65536]{1,0:T(4,128)}, f32[3,4096]{1,0:T(4,128)}) custom-call(bf16[384,256]{1,0:T(8,128)(2,1)} %get-tuple-element.6.refs_0_, f8e4m3fn[384,512]{1,0:T(32,128)(4,1)} %get-tuple-element.7.refs_1_, f32[8,128]{1,0:T(8,128)} %get-tuple-element.8.refs_2_, f32[9,4096]{1,0:T(8,128)} %get-tuple-element.9.refs_3_, s32[1,65536]{1,0:T(1,128)} %bitcast.8, ...), custom_call_target="tpu_custom_call" | custom-call | tf_op jit(solution)/shard_map/kick/pallas_call | solution.py:287

commit v3 on v2

--- a/solution.py
+++ b/solution.py
@@ -21,21 +21,21 @@
     return hi, (table - hi.astype(np.float64)).astype(jnp.bfloat16)
 
 
-def row_places():
-    layer, y = np.full(PAD, -1), np.zeros(PAD, int)
-    layer[:192], y[:192] = np.arange(192) // 32, np.arange(192) % 32
-    for side in range(2):
-        layer[192 + 8 * side : 198 + 8 * side] = np.arange(6)
-        y[192 + 8 * side : 200 + 8 * side] = 33 * side - 1
-    return layer, y
+def y_places():
+    y = np.full(PAD, -1)
+    y[:128] = np.arange(128)
+    for r in range(N_ROW):
+        for side in range(2):
+            first = 128 + 16 * r + 8 * side
+            y[first : first + 6] = 32 * r + 33 * side - 1
+    return y
 
 
 def tables():
     wave = np.arange(256)
-    layer, y = row_places()
-    yg = 32 * np.arange(N_ROW)[:, None] + y[None]
-    live = ((layer >= 0)[None] & (yg >= 0) & (yg < 128)).reshape(-1, 1)
-    angle = 2 * np.pi / 256 * (yg.reshape(-1, 1) * wave % 256)
+    y = y_places()[:, None]
+    angle = 2 * np.pi / 256 * (y * wave % 256)
+    live = (y >= 0) & (y < 128)
     ey = np.concatenate([np.cos(angle), np.sin(angle)], axis=1) * live
     zg = (4 * np.arange(N_COL)[None] + np.arange(6)[:, None] - 1).reshape(-1)
     live = ((zg >= 0) & (zg < 128))[None]
@@ -303,11 +303,6 @@
     )(*ops)
 
 
-def layer_of(shape):
-    lane = lax.broadcasted_iota(I32, shape, 1)
-    return jnp.where(lane < 192, lane // 32, jnp.where(lane < ROWS, lane % 8, 6))
-
-
 def green_into(green_ref, h_ref, first):
     index = lax.broadcasted_iota(I32, (256, 256), 0) + lax.broadcasted_iota(I32, (256, 256), 1)
     mirror = ((index == 0) | (index == 256)).astype(BF)
@@ -331,17 +326,33 @@
             h_ref[a, 1] = green_ref[a, 1, 0].astype(F32) - flip(green_ref[a, 1, 1])
 
 
+def lanes(rows):
+    return lax.broadcasted_iota(I32, (rows, 128), 1)
+
+
+def turn(v, by):
+    by = by % 128
+    return pltpu.roll(v, by, 1) if by else v
+
+
 def forward_into(got_ref, ey, ez, lhs_ref, s_ref, first):
-    layer = layer_of((N_COL, PAD))
+    lane = lanes(N_COL)
     for part in range(2):
+        inner = [jnp.zeros((N_COL, 128), F32)] * 6
+        rims = jnp.zeros((N_COL, 128), F32)
         for r in range(N_ROW):
             rows = slice(32 * r, 32 * r + 32)
-            both = jnp.concatenate([got_ref[rows, 2 * part, :], got_ref[rows, 2 * part + 1, :]], axis=1)
+            low, high = got_ref[rows, 2 * part, :], got_ref[rows, 2 * part + 1, :]
             for ze in range(6):
-                hi, lo = split(jnp.where(layer == ze, both, 0.0))
-                where = slice(192 * part + 32 * ze, 192 * part + 32 * ze + 32)
-                lhs_ref[0, where, PAD * r : PAD * r + PAD] = hi
-                lhs_ref[1, where, PAD * r : PAD * r + PAD] = lo
+                moved = turn(low if ze < 4 else high, 32 * (r - ze % 4))
+                inner[ze] = jnp.where(lane // 32 == r, moved, inner[ze])
+            rims = jnp.where(lane // 16 == r, turn(high, 16 * r - 64), rims)
+        for ze in range(6):
+            where = slice(192 * part + 32 * ze, 192 * part + 32 * ze + 32)
+            for k, v in enumerate((inner[ze], jnp.where(lane % 8 == ze, rims, 0.0))):
+                hi, lo = split(v)
+                lhs_ref[0, where, 128 * k : 128 * k + 128] = hi
+                lhs_ref[1, where, 128 * k : 128 * k + 128] = lo
     u = dot3((lhs_ref[0], lhs_ref[1]), (ey[0][...], ey[1][...]))
     re_c, re_s, im_c, im_s = u[:192, :256], u[:192, 256:], u[192:, :256], u[192:, 256:]
     ezs = (ez[0][...], ez[1][...])
@@ -360,8 +371,7 @@
         s_ref[0], s_ref[1] = forward(re_c + im_s, im_c - re_s)
 
 
-def back_into(a, h_ref, s_ref, q_ref, zt, ey, out_ref, first):
-    layer = layer_of((N_COL, PAD))
+def back_into(a, h_ref, s_ref, q_ref, zt, ey, out_ref, at, rim_ref, first):
     a_re = s_ref[0] * h_ref[a, 0] - s_ref[1] * h_ref[a, 1]
     a_im = s_ref[0] * h_ref[a, 1] + s_ref[1] * h_ref[a, 0]
     q_ref[0], q_ref[1] = a_re, a_im
@@ -375,19 +385,34 @@
 
     q = split(jnp.concatenate([q_ref[0], q_ref[1]], axis=1))
     v = dot3((zt[0][...], zt[1][...]), q)
-    v = jnp.concatenate([v[:192, :256] - v[192:, 256:], v[:192, 256:] + v[192:, :256]], axis=0)
-    v = split(v)
+    v = split(jnp.concatenate([v[:192, :256] - v[192:, 256:], v[:192, 256:] + v[192:, :256]], axis=0))
+    cos = dot3(v, (ey[0][:, :256], ey[1][:, :256]), ((1,), (1,)))
+    sin = dot3(v, (ey[0][:, 256:], ey[1][:, 256:]), ((1,), (1,)))
+    w = (cos[:192] - sin[192:], cos[192:] + sin[:192])
+    lane = lanes(N_COL)
+    rims = []
+    for part in range(2):
+        rim = jnp.zeros((N_COL, 128), F32)
+        for ze in range(6):
+            rim = jnp.where(lane % 8 == ze, w[part][32 * ze : 32 * ze + 32, 128:], rim)
+        rims.append(rim)
     for r in range(N_ROW):
-        rows = slice(PAD * r, PAD * r + PAD)
-        cos = dot3(v, (ey[0][rows, :256], ey[1][rows, :256]), ((1,), (1,)))
-        sin = dot3(v, (ey[0][rows, 256:], ey[1][rows, 256:]), ((1,), (1,)))
-        w = (cos[:192] - sin[192:], cos[192:] + sin[:192])
+        rows = slice(32 * r, 32 * r + 32)
+        shared = jnp.zeros((N_COL, 128), F32)
         for part in range(2):
-            mine = jnp.zeros((N_COL, PAD), F32)
+            mine = jnp.zeros((N_COL, 128), F32)
             for ze in range(6):
-                mine = jnp.where(layer == ze, w[part][32 * ze : 32 * ze + 32], mine)
-            for half in range(2):
-                out_ref[a, 32 * r : 32 * r + 32, 2 * part + half, :] = mine[:, 128 * half : 128 * half + 128]
+                to = ze if ze < 4 else ze - 4 + 2 * part
+                moved = turn(w[part][32 * ze : 32 * ze + 32, :128], 32 * (to - r))
+                if ze < 4:
+                    mine = jnp.where(lane // 32 == to, moved, mine)
+                else:
+                    shared = jnp.where(lane // 32 == to, moved, shared)
+            out_ref[rows, at + part, :] = mine
+            to = 2 * a + part
+            old = rim_ref[rows]
+            rim_ref[rows] = jnp.where(lane // 16 == to, turn(rims[part], 16 * (to - r)), old)
+        out_ref[rows, at + 2, :] = shared
 
 
 MESH = pl.DeviceIdType.MESH
@@ -397,10 +422,11 @@
 def field_kernel(*refs, n):
     hbm, (ft_ref, f8_ref, scale_ref, moved_ref) = refs[:N_IN], refs[N_IN : N_IN + 4]
     held = refs[N_IN + 4 : 2 * N_IN + 4]
-    (lhs_p, pack_s, pack_r, a_ref, b_ref, acc_ref, send1, recv1, h_ref, lhs_f, s_ref, q_ref, send2, recv2) = refs[
-        2 * N_IN + 4 : 2 * N_IN + 18
+    (lhs_p, pack_s, pack_r, a_ref, b_ref, acc_ref, send1, recv1, h_ref, lhs_f, s_ref, q_ref, *late) = refs[
+        2 * N_IN + 4 : 2 * N_IN + 21
     ]
-    in_sem, own_sem, ss_m, rs_m, ss_1, rs_1, ss_2, rs_2 = refs[2 * N_IN + 18 :]
+    send2, recv2, rim_ref = late[:2], late[2:4], late[4]
+    meet, in_sem, own_sem, ss_m, rs_m, ss_1, rs_1, ss_2, rs_2 = refs[2 * N_IN + 21 :]
     row, col = lax.axis_index("row"), lax.axis_index("col")
     me = row * N_COL + col
     first = me == 0
@@ -414,11 +440,16 @@
 
     barrier = pltpu.get_barrier_semaphore()
 
-    def greet(i, _):
-        pl.semaphore_signal(barrier, inc=1, device_id=device((me + i) & 127), device_id_type=MESH)
+    def greet_row(sem):
+        for i in range(1, N_ROW):
+            pl.semaphore_signal(sem, inc=1, device_id=((row + i) & 3, col), device_id_type=MESH)
+
+    def greet_col(i, _):
+        pl.semaphore_signal(barrier, inc=1, device_id=(row, (col + i) & 31), device_id_type=MESH)
         return 0
 
-    lax.fori_loop(1, SLOTS, greet, 0)
+    greet_row(barrier)
+    lax.fori_loop(1, N_COL, greet_col, 0)
     acc_ref[...] = jnp.zeros_like(acc_ref)
 
     for copy in copies[:6]:
@@ -446,7 +477,8 @@
         return 0
 
     lax.fori_loop(0, steps // 2, resident, 0)
-    pl.semaphore_wait(barrier, SLOTS - 1)
+    pl.semaphore_wait(barrier, N_ROW - 1 + N_COL - 1)
+    greet_row(meet)
 
     def send_migrants(i, _):
         c = (col + i) & 31
@@ -537,17 +569,30 @@
             device_id_type=MESH,
         ).wait()
 
+    pl.semaphore_wait(meet, N_ROW - 1)
     own = exchange(send1, recv1, ss_1, rs_1, own_sem.at[1])
     green_into(green_ref, h_ref, first)
     finish(own, send1, recv1, ss_1, rs_1)
     forward_into(recv1, ey, ez, lhs_f, s_ref, first)
-    owns = []
+    rim_ref[...] = jnp.zeros_like(rim_ref)
+    back_into(0, h_ref, s_ref, q_ref, zt, ey, send2[0], 0, rim_ref, first)
+    back_into(1, h_ref, s_ref, q_ref, zt, ey, send2[0], 3, rim_ref, first)
+    owns = [exchange(send2[0], recv2[0], ss_2.at[0], rs_2.at[0], own_sem.at[2])]
+    back_into(2, h_ref, s_ref, q_ref, zt, ey, send2[1], 0, rim_ref, first)
+    send2[1][:, 3, :] = rim_ref[...]
+    owns.append(exchange(send2[1], recv2[1], ss_2.at[1], rs_2.at[1], own_sem.at[3]))
+    for k in range(2):
+        finish(owns[k], send2[k], recv2[k], ss_2.at[k], rs_2.at[k])
+    lane = lanes(SLOTS)
+    rims = recv2[1][:, 3, :]
     for a in range(3):
-        back_into(a, h_ref, s_ref, q_ref, zt, ey, send2, first)
-        owns.append(exchange(send2.at[a], recv2.at[a], ss_2.at[a], rs_2.at[a], own_sem.at[2 + a]))
-    for a in range(3):
-        finish(owns[a], send2.at[a], recv2.at[a], ss_2.at[a], rs_2.at[a])
-        parts = [jnp.concatenate([recv2[a, :, 2 * part, :], recv2[a, :, 2 * part + 1, :]], axis=1) for part in range(2)]
+        from_ref, at = recv2[a // 2], 3 * (a % 2)
+        shared = from_ref[:, at + 2, :]
+        parts = []
+        for part in range(2):
+            rest = jnp.where(lane < 80, turn(rims, 64 - 16 * (2 * a + part)), 0.0)
+            rest = jnp.where(lane < 64, turn(shared, -64 * part), rest)
+            parts.append(jnp.concatenate([from_ref[:, at + part, :], rest], axis=1))
         field = dot3((xi[0][...], xi[1][...]), split(jnp.concatenate(parts, axis=0)))
         top = jnp.max(jnp.max(jnp.abs(field), axis=0, keepdims=True), axis=1, keepdims=True)
         top = jnp.maximum(top, 1e-30)
@@ -561,7 +606,7 @@
     scale_ref[3:] = jnp.zeros((5, 128), F32)
 
 
-def field_of(operands, blk=2048, n=512):
+def field_of(operands, blk=4096, n=512):
     ops = [o.reshape(1, -1) if o.ndim == 1 else o for o in operands]
     assert len(ops) == N_IN
     cap = 128
@@ -588,19 +633,23 @@
             pltpu.VMEM((SLOTS, 4, 128), F32),
             pltpu.VMEM((SLOTS, 4, 128), F32),
             pltpu.VMEM((3, 4, 256, 256), F32),
-            pltpu.VMEM((2, 384, 1024), BF),
+            pltpu.VMEM((2, 384, PAD), BF),
             pltpu.VMEM((4, 256, 256), F32),
             pltpu.VMEM((2, 256, 256), F32),
-            pltpu.VMEM((3, SLOTS, 4, 128), F32),
-            pltpu.VMEM((3, SLOTS, 4, 128), F32),
+            pltpu.VMEM((SLOTS, 6, 128), F32),
+            pltpu.VMEM((SLOTS, 4, 128), F32),
+            pltpu.VMEM((SLOTS, 6, 128), F32),
+            pltpu.VMEM((SLOTS, 4, 128), F32),
+            pltpu.VMEM((SLOTS, 128), F32),
+            pltpu.SemaphoreType.REGULAR,
             dma((N_IN,)),
             dma((5,)),
             dma(()),
             dma(()),
             dma(()),
             dma(()),
-            dma((3,)),
-            dma((3,)),
+            dma((2,)),
+            dma((2,)),
         ],
         compiler_params=pltpu.CompilerParams(vmem_limit_bytes=BIG, has_side_effects=True, collective_id=0),
     )(*ops)

time: 104 us -> 98 us (0.942)
  Pallas kernels: 103 us -> 97 us
    pallas_call x1, Pallas kernels: 63.7 us -> 58.1 us  [field_of(): pl.pallas_call(functools.partial(field_kernel, n=n), name='field', out_sh...]
where the time goes in v3:
time: 98 us; the launch traced here: 97.8 us
  Pallas kernels  97 us (99%)
    pallas_call x1, Pallas kernels, field_of(): pl.pallas_call(functools.partial(field_kernel, n=n), name='field', out_sh...  58.1 us
    pallas_call x1, Pallas kernels, kick(): pl.pallas_call(functools.partial(kick_kernel, n=n), name='kick', out_shap...  38.9 us

profile of v3, /device:TPU:1, one launch (start us, length us, event | category | flops | bytes accessed | tf_op | source)
XLA Modules:
  0.0 97.8 jit_solution(17112817110864008494)
XLA Ops:
  0.6 58.1 %field.1 = (bf16[384,256]{1,0:T(8,128)(2,1)}, f8e4m3fn[384,512]{1,0:T(32,128)(4,1)}, f32[8,128]{1,0:T(8,128)}, f32[9,4096]{1,0:T(8,128)}) custom-call(s32[1,2048]{1,0:T(1,128)} %bitcast.13, s32[1,2048]{1,0:T(1,128)} %bitcast.14, s32[1,2048]{1,0:T(1,128)} %bitcast.15, f32[3,2048]{1,0:T(4,128)} %refs_3_.1, f32[1,2048]{1,0:T(1,128)} %bitcast.16, ...), custom_call_target="tpu_custom_call" | custom-call | tf_op jit(solution)/shard_map/field/pallas_call | solution.py:614
  58.8 38.9 %kick.1 = (f32[3,65536]{1,0:T(4,128)}, f32[3,4096]{1,0:T(4,128)}) custom-call(bf16[384,256]{1,0:T(8,128)(2,1)} %get-tuple-element.6.refs_0_, f8e4m3fn[384,512]{1,0:T(32,128)(4,1)} %get-tuple-element.7.refs_1_, f32[8,128]{1,0:T(8,128)} %get-tuple-element.8.refs_2_, f32[9,4096]{1,0:T(8,128)} %get-tuple-element.9.refs_3_, s32[1,65536]{1,0:T(1,128)} %bitcast.8, ...), custom_call_target="tpu_custom_call" | custom-call | tf_op jit(solution)/shard_map/kick/pallas_call | solution.py:287

commit v4 on v3

--- a/solution.py
+++ b/solution.py
@@ -217,8 +217,8 @@
 
 
 def kick_kernel(*refs, n):
-    hbm, (out_hbm, migrant_ref), held = refs[:9], refs[9:11], refs[11:20]
-    out_ref, w_ref, w8_ref, made_sem, in_sem, out_sem = refs[20:]
+    hbm, (out_hbm, migrant_hbm), held = refs[:9], refs[9:11], refs[11:20]
+    out_ref, migrant_ref, w_ref, w8_ref, made_sem, in_sem, out_sem, migrant_sem = refs[20:]
     made = [pltpu.make_async_copy(hbm[i], held[i], made_sem.at[i]) for i in range(4)]
     for copy in made:
         copy.start()
@@ -251,6 +251,8 @@
         return 0
 
     lax.fori_loop(0, moved_ref.shape[1] // blk, migrants, 0)
+    migrant_out = pltpu.make_async_copy(migrant_ref, migrant_hbm, migrant_sem)
+    migrant_out.start()
     for copy in copies[0]:
         copy.wait()
 
@@ -278,25 +280,28 @@
         return 0
 
     lax.fori_loop(0, total // blk, residents, 0)
+    migrant_out.wait()
     pltpu.make_async_copy(out_ref, out_hbm, out_sem).wait()
 
 
 def kick(tables_of, moved, cell, corner, frac, q, mom, blk=4096, n=256):
     ops = [*tables_of, moved, cell.reshape(1, -1), corner.reshape(1, -1), frac, q.reshape(1, -1), mom]
-    vmem, hbm = (pl.BlockSpec(memory_space=s) for s in (pltpu.VMEM, pltpu.MemorySpace.HBM))
+    hbm = pl.BlockSpec(memory_space=pltpu.MemorySpace.HBM)
     return pl.pallas_call(
         functools.partial(kick_kernel, n=n),
         name="kick",
         out_shape=(jax.ShapeDtypeStruct(mom.shape, F32), jax.ShapeDtypeStruct((3, moved.shape[1]), F32)),
         in_specs=[hbm] * 9,
-        out_specs=(hbm, vmem),
+        out_specs=(hbm, hbm),
         scratch_shapes=[pltpu.VMEM(o.shape, o.dtype) for o in ops]
         + [
             pltpu.VMEM(mom.shape, F32),
+            pltpu.VMEM((3, moved.shape[1]), F32),
             pltpu.VMEM((PAD, blk), BF),
             pltpu.VMEM((2 * PAD, blk), F8),
             pltpu.SemaphoreType.DMA((4,)),
             pltpu.SemaphoreType.DMA((2, 5)),
+            pltpu.SemaphoreType.DMA(()),
             pltpu.SemaphoreType.DMA(()),
         ],
         compiler_params=pltpu.CompilerParams(vmem_limit_bytes=BIG),
@@ -420,13 +425,14 @@
 
 
 def field_kernel(*refs, n):
-    hbm, (ft_ref, f8_ref, scale_ref, moved_ref) = refs[:N_IN], refs[N_IN : N_IN + 4]
+    hbm, (ft_out, f8_out, scale_out, moved_out) = refs[:N_IN], refs[N_IN : N_IN + 4]
     held = refs[N_IN + 4 : 2 * N_IN + 4]
     (lhs_p, pack_s, pack_r, a_ref, b_ref, acc_ref, send1, recv1, h_ref, lhs_f, s_ref, q_ref, *late) = refs[
-        2 * N_IN + 4 : 2 * N_IN + 21
+        2 * N_IN + 4 : 2 * N_IN + 25
     ]
     send2, recv2, rim_ref = late[:2], late[2:4], late[4]
-    meet, in_sem, own_sem, ss_m, rs_m, ss_1, rs_1, ss_2, rs_2 = refs[2 * N_IN + 21 :]
+    ft_ref, f8_ref, scale_ref, moved_ref = late[5:]
+    meet, in_sem, own_sem, ss_m, rs_m, ss_1, rs_1, ss_2, rs_2, out_sem = refs[2 * N_IN + 25 :]
     row, col = lax.axis_index("row"), lax.axis_index("col")
     me = row * N_COL + col
     first = me == 0
@@ -435,7 +441,7 @@
         return (d >> 5, d & 31)
 
     copies = [pltpu.make_async_copy(h, v, in_sem.at[i]) for i, (h, v) in enumerate(zip(hbm, held))]
-    for copy in copies:
+    for copy in copies[:6]:
         copy.start()
 
     barrier = pltpu.get_barrier_semaphore()
@@ -449,7 +455,9 @@
         return 0
 
     greet_row(barrier)
-    lax.fori_loop(1, N_COL, greet_col, 0)
+    lax.fori_loop(1, N_COL, greet_col, 0, unroll=8)
+    for copy in copies[6:]:
+        copy.start()
     acc_ref[...] = jnp.zeros_like(acc_ref)
 
     for copy in copies[:6]:
@@ -492,7 +500,7 @@
         ).start()
         return 0
 
-    lax.fori_loop(1, N_COL, send_migrants, 0)
+    lax.fori_loop(1, N_COL, send_migrants, 0, unroll=8)
     own = pltpu.make_async_copy(pack_s.at[col], pack_r.at[col], own_sem.at[0])
     own.start()
     lax.fori_loop(steps // 2, steps, resident, 0)
@@ -508,6 +516,8 @@
     ).wait()
     for s in range(N_COL):
         moved_ref[:, 128 * s : 128 * s + 128] = pack_r[s]
+    leaving = [pltpu.make_async_copy(moved_ref, moved_out, out_sem.at[0])]
+    leaving[0].start()
 
     def migrant(i, _):
         def rows(s):
@@ -552,7 +562,7 @@
             ).start()
             return 0
 
-        lax.fori_loop(1, SLOTS, go, 0)
+        lax.fori_loop(1, SLOTS, go, 0, unroll=8)
         own = pltpu.make_async_copy(src.at[me], dst.at[me], own_at)
         own.start()
         return own
@@ -603,7 +613,14 @@
         f8_ref[here, :PAD] = ((field - hi) * 65536.0).astype(F8)
         f8_ref[here, PAD:] = (hi * 16.0).astype(F8)
         scale_ref[a : a + 1] = jnp.broadcast_to(top * (1.0 / 65536.0), (1, 128))
+        for i, (v, o) in enumerate(((ft_ref, ft_out), (f8_ref, f8_out))):
+            leaving.append(pltpu.make_async_copy(v.at[here], o.at[here], out_sem.at[1 + 2 * a + i]))
+            leaving[-1].start()
     scale_ref[3:] = jnp.zeros((5, 128), F32)
+    leaving.append(pltpu.make_async_copy(scale_ref, scale_out, out_sem.at[7]))
+    leaving[-1].start()
+    for copy in leaving:
+        copy.wait()
 
 
 def field_of(operands, blk=4096, n=512):
@@ -621,7 +638,7 @@
             jax.ShapeDtypeStruct((9, N_COL * cap), F32),
         ),
         in_specs=[pl.BlockSpec(memory_space=pltpu.MemorySpace.HBM)] * N_IN,
-        out_specs=(pl.BlockSpec(memory_space=pltpu.VMEM),) * 4,
+        out_specs=(pl.BlockSpec(memory_space=pltpu.MemorySpace.HBM),) * 4,
         scratch_shapes=[pltpu.VMEM(o.shape, o.dtype) for o in ops]
         + [
             pltpu.VMEM((3 * 512, ops[0].shape[1]), BF),
@@ -641,6 +658,10 @@
             pltpu.VMEM((SLOTS, 6, 128), F32),
             pltpu.VMEM((SLOTS, 4, 128), F32),
             pltpu.VMEM((SLOTS, 128), F32),
+            pltpu.VMEM((384, PAD), BF),
+            pltpu.VMEM((384, 2 * PAD), F8),
+            pltpu.VMEM((8, 128), F32),
+            pltpu.VMEM((9, N_COL * cap), F32),
             pltpu.SemaphoreType.REGULAR,
             dma((N_IN,)),
             dma((5,)),
@@ -650,6 +671,7 @@
             dma(()),
             dma((2,)),
             dma((2,)),
+            dma((8,)),
         ],
         compiler_params=pltpu.CompilerParams(vmem_limit_bytes=BIG, has_side_effects=True, collective_id=0),
     )(*ops)

time: 98 us -> 96.6 us (0.986)
  Pallas kernels: 97 us -> 95.7 us
where the time goes in v4:
time: 96.6 us; the launch traced here: 96.5 us
  Pallas kernels  95.7 us (99%)
    pallas_call x1, Pallas kernels, field_of(): pl.pallas_call(functools.partial(field_kernel, n=n), name='field', out_sh...  57.4 us
    pallas_call x1, Pallas kernels, kick(): pl.pallas_call(functools.partial(kick_kernel, n=n), name='kick', out_shap...  38.3 us

profile of v4, /device:TPU:1, one launch (start us, length us, event | category | flops | bytes accessed | tf_op | source)
XLA Modules:
  0.0 96.5 jit_solution(2599836500983980776)
XLA Ops:
  0.6 57.4 %field.1 = (bf16[384,256]{1,0:T(8,128)(2,1)}, f8e4m3fn[384,512]{1,0:T(32,128)(4,1)}, f32[8,128]{1,0:T(8,128)}, f32[9,4096]{1,0:T(8,128)}) custom-call(s32[1,2048]{1,0:T(1,128)} %bitcast.13, s32[1,2048]{1,0:T(1,128)} %bitcast.14, s32[1,2048]{1,0:T(1,128)} %bitcast.15, f32[3,2048]{1,0:T(4,128)} %refs_3_.1, f32[1,2048]{1,0:T(1,128)} %bitcast.16, ...), custom_call_target="tpu_custom_call" | custom-call | tf_op jit(solution)/shard_map/field/pallas_call | solution.py:631
  58.0 38.3 %kick.1 = (f32[3,65536]{1,0:T(4,128)}, f32[3,4096]{1,0:T(4,128)}) custom-call(bf16[384,256]{1,0:T(8,128)(2,1)} %get-tuple-element.6.refs_0_, f8e4m3fn[384,512]{1,0:T(32,128)(4,1)} %get-tuple-element.7.refs_1_, f32[8,128]{1,0:T(8,128)} %get-tuple-element.8.refs_2_, f32[9,4096]{1,0:T(8,128)} %get-tuple-element.9.refs_3_, s32[1,65536]{1,0:T(1,128)} %bitcast.8, ...), custom_call_target="tpu_custom_call" | custom-call | tf_op jit(solution)/shard_map/kick/pallas_call | solution.py:290

commit v5 on v4

--- a/solution.py
+++ b/solution.py
@@ -240,17 +240,13 @@
     for copy in made:
         copy.wait()
 
-    def migrants(i, _):
-        for s in range(blk // n):
-            here = pl.ds(pl.multiple_of(i * blk + s * n, n), n)
-            got = moved_ref[:, here]
-            rows = (got[7:8].astype(I32), got[8:9].astype(I32), got[0:1], got[1:2], got[2:3], got[3:4])
-            kicks = chunk(pl.ds(s * n, n), n, rows)
-            for a in range(3):
-                migrant_ref[a : a + 1, here] = got[4 + a : 5 + a] + kicks[a] * scale_ref[a : a + 1, 0:1]
-        return 0
-
-    lax.fori_loop(0, moved_ref.shape[1] // blk, migrants, 0)
+    for s in range(moved_ref.shape[1] // n):
+        here = pl.ds(s * n, n)
+        got = moved_ref[:, here]
+        rows = (got[7:8].astype(I32), got[8:9].astype(I32), got[0:1], got[1:2], got[2:3], got[3:4])
+        kicks = chunk(here, n, rows)
+        for a in range(3):
+            migrant_ref[a : a + 1, here] = got[4 + a : 5 + a] + kicks[a] * scale_ref[a : a + 1, 0:1]
     migrant_out = pltpu.make_async_copy(migrant_ref, migrant_hbm, migrant_sem)
     migrant_out.start()
     for copy in copies[0]:
@@ -284,7 +280,7 @@
     pltpu.make_async_copy(out_ref, out_hbm, out_sem).wait()
 
 
-def kick(tables_of, moved, cell, corner, frac, q, mom, blk=4096, n=256):
+def kick(tables_of, moved, cell, corner, frac, q, mom, blk=8192, n=256):
     ops = [*tables_of, moved, cell.reshape(1, -1), corner.reshape(1, -1), frac, q.reshape(1, -1), mom]
     hbm = pl.BlockSpec(memory_space=pltpu.MemorySpace.HBM)
     return pl.pallas_call(
@@ -466,22 +462,24 @@
     for copy in copies[6:10]:
         copy.wait()
     cell_ref, corner_ref, frac_ref, q_in = held[6:10]
-    blk = a_ref.shape[1]
-    steps = cell_ref.shape[1] // blk
+    blk = a_ref.shape[2]
+    steps = cell_ref.shape[1] // (2 * blk)
 
     def resident(i, _):
-        def rows(s):
-            here = pl.ds(pl.multiple_of(i * blk + s * n, n), n)
-            return (
-                cell_ref[:, here],
-                corner_ref[:, here],
-                frac_ref[0:1, here],
-                frac_ref[1:2, here],
-                frac_ref[2:3, here],
-                q_in[:, here],
-            )
-
-        deposit_block(rows, a_ref, b_ref, acc_ref, n)
+        for k in range(2):
+
+            def rows(s, k=k):
+                here = pl.ds(pl.multiple_of((2 * i + k) * blk + s * n, n), n)
+                return (
+                    cell_ref[:, here],
+                    corner_ref[:, here],
+                    frac_ref[0:1, here],
+                    frac_ref[1:2, here],
+                    frac_ref[2:3, here],
+                    q_in[:, here],
+                )
+
+            deposit_block(rows, a_ref.at[k], b_ref.at[k], acc_ref, n)
         return 0
 
     lax.fori_loop(0, steps // 2, resident, 0)
@@ -532,7 +530,7 @@
                 got[3:4],
             )
 
-        deposit_block(rows, a_ref, b_ref, acc_ref, n)
+        deposit_block(rows, a_ref.at[0], b_ref.at[0], acc_ref, n)
         return 0
 
     lax.fori_loop(0, moved_ref.shape[1] // blk, migrant, 0)
@@ -644,8 +642,8 @@
             pltpu.VMEM((3 * 512, ops[0].shape[1]), BF),
             pltpu.VMEM((N_COL, 9, cap), F32),
             pltpu.VMEM((N_COL, 9, cap), F32),
-            pltpu.VMEM((2 * ROWS, blk), BF),
-            pltpu.VMEM((256, blk), BF),
+            pltpu.VMEM((2, 2 * ROWS, blk), BF),
+            pltpu.VMEM((2, 256, blk), BF),
             pltpu.VMEM((2 * ROWS, 256), F32),
             pltpu.VMEM((SLOTS, 4, 128), F32),
             pltpu.VMEM((SLOTS, 4, 128), F32),

time: 96.6 us -> 94.1 us (0.974)
  Pallas kernels: 95.7 us -> 93.2 us
    pallas_call x1, Pallas kernels: 57.4 us -> 55.7 us  [field_of(): pl.pallas_call(functools.partial(field_kernel, n=n), name='field', out_sh...]
where the time goes in v5:
time: 94.1 us; the launch traced here: 94 us
  Pallas kernels  93.2 us (99%)
    pallas_call x1, Pallas kernels, field_of(): pl.pallas_call(functools.partial(field_kernel, n=n), name='field', out_sh...  55.7 us
    pallas_call x1, Pallas kernels, kick(): pl.pallas_call(functools.partial(kick_kernel, n=n), name='kick', out_shap...  37.5 us

profile of v5, /device:TPU:1, one launch (start us, length us, event | category | flops | bytes accessed | tf_op | source)
XLA Modules:
  0.0 94.0 jit_solution(4255277120066450527)
XLA Ops:
  0.6 55.7 %field.1 = (bf16[384,256]{1,0:T(8,128)(2,1)}, f8e4m3fn[384,512]{1,0:T(32,128)(4,1)}, f32[8,128]{1,0:T(8,128)}, f32[9,4096]{1,0:T(8,128)}) custom-call(s32[1,2048]{1,0:T(1,128)} %bitcast.13, s32[1,2048]{1,0:T(1,128)} %bitcast.14, s32[1,2048]{1,0:T(1,128)} %bitcast.15, f32[3,2048]{1,0:T(4,128)} %refs_3_.1, f32[1,2048]{1,0:T(1,128)} %bitcast.16, ...), custom_call_target="tpu_custom_call" | custom-call | tf_op jit(solution)/shard_map/field/pallas_call | solution.py:629
  56.3 37.5 %kick.1 = (f32[3,65536]{1,0:T(4,128)}, f32[3,4096]{1,0:T(4,128)}) custom-call(bf16[384,256]{1,0:T(8,128)(2,1)} %get-tuple-element.6.refs_0_, f8e4m3fn[384,512]{1,0:T(32,128)(4,1)} %get-tuple-element.7.refs_1_, f32[8,128]{1,0:T(8,128)} %get-tuple-element.8.refs_2_, f32[9,4096]{1,0:T(8,128)} %get-tuple-element.9.refs_3_, s32[1,65536]{1,0:T(1,128)} %bitcast.8, ...), custom_call_target="tpu_custom_call" | custom-call | tf_op jit(solution)/shard_map/kick/pallas_call | solution.py:286
